TPU v7x, 256 devices: a whole 4x4x8 slice. The times are simulated.
256 devices in a mesh: row: 32 (over z_lo, x, core), col: 8 (over y, z_hi).
Axes of the slice: x: 4, y: 4, z: 8 (z_hi: 2, z_lo: 4; z = z_hi * 4 + z_lo), core: 2. Of those that a mesh axis runs over, the one named last changes fastest.
Arguments:
- occ_coef: bfloat16 [24576, 4096], P(('row', 'col')), may hold values from -0.25 to 0.25
- vir_coef: bfloat16 [24576, 10240], P(('row', 'col')), may hold values from -0.15811388 to 0.15811388
- occ_weight: float32 [4096], replicated, may hold values from 0.05 to 1
- vir_weight: float32 [10240], replicated, may hold values from 0.02 to 1
- three_center: bfloat16 [2048, 128, 256], P(('row', 'col')), may hold values from -0.59765625 to 0.59765625
- pair_blocks: int32 [2048, 3], P(('row', 'col')), may hold values from 0 to 1535, as said below
- send_pairs: int32 [8192, 1], P(('row', 'col')), may hold values from 0 to 7, as said below
- partners: int32 [2048, 12], P(('row', 'col')), may hold values from 0 to 31, as said below
- partner_blocks: int32 [2048, 12, 3], P(('row', 'col')), may hold values from 0 to 1535, as said below
Outputs:
- chi_slab: float32 [512, 512], P('row', 'col')
Inputs may be any that keep to these rules, and one draw needn't show every extreme that they name: pair_blocks[j, 0] and pair_blocks[j, 1] lie in [d * 6, (d + 1) * 6) with d = j // 8; pair_blocks[j, 2] is below 4. `send_pairs`: local pair indices. `partners`: every slot is named by some pair of each device. partner_blocks[j, t] equals pair_blocks[partner[j, t]].
All inputs are finite; a program needn't handle non-finite values.
Results may differ from a plain program's by a relative error of at most 0.0045.
Values may be sent and summed in bfloat16 or wider, within the bound.
No kernel may reach another device: no remote copies, remote signals or barrier semaphores. Data moves between devices by JAX's collectives and lax.ppermute only.
A program may use at most 128 MiB of HBM per device.

v0:
```python
import jax
import jax.numpy as jnp
from jax import lax
from jax.sharding import PartitionSpec as P

BB = 16
AB = 128
NNB = 12
NAB = 4


def body(
    occ_coef,
    vir_coef,
    occ_weight,
    vir_weight,
    three_center,
    pair_blocks,
    send_pairs,
    partners,
    partner_blocks,
):
    row_count = lax.axis_size("row")
    col_count = lax.axis_size("col")
    occ_width = occ_coef.shape[1]
    vir_width = vir_coef.shape[1]
    local_blocks = occ_coef.shape[0] // BB
    device_rank = lax.axis_index("row") * col_count + lax.axis_index("col")
    first_block = device_rank * local_blocks
    scaled_occ = (occ_coef.astype(jnp.float32) * occ_weight[None, :]).astype(jnp.bfloat16)
    scaled_vir = (vir_coef.astype(jnp.float32) * vir_weight[None, :]).astype(jnp.bfloat16)
    picked = send_pairs.reshape(-1)
    sent_ids = pair_blocks[picked]
    out_blocks = three_center[picked]
    out_occ = occ_coef.reshape(local_blocks, BB, occ_width)[sent_ids[:, 0] - first_block]
    out_vir = vir_coef.reshape(local_blocks, BB, vir_width)[sent_ids[:, 1] - first_block]
    received, recv_occ, recv_vir = (
        lax.all_to_all(out_blocks, "row", split_axis=0, concat_axis=0, tiled=True),
        lax.all_to_all(out_occ, "row", split_axis=0, concat_axis=0, tiled=True),
        lax.all_to_all(out_vir, "row", split_axis=0, concat_axis=0, tiled=True),
    )
    slot_total = recv_occ.shape[0]
    dens_occ = jnp.einsum(
        "mi,li->ml",
        scaled_occ,
        recv_occ.reshape(slot_total * BB, occ_width),
        preferred_element_type=jnp.float32,
    ).astype(jnp.bfloat16)
    dens_vir = jnp.einsum(
        "mi,li->ml",
        scaled_vir,
        recv_vir.reshape(slot_total * BB, vir_width),
        preferred_element_type=jnp.float32,
    ).astype(jnp.bfloat16)
    occ_grid = dens_occ.reshape(local_blocks, BB, slot_total, BB).transpose(0, 2, 1, 3)
    vir_grid = dens_vir.reshape(local_blocks, BB, slot_total, BB).transpose(0, 2, 1, 3)
    group_size = 4
    turn_count = three_center.shape[0] // group_size
    aux_total = NAB * AB
    inputs = (
        three_center.reshape(turn_count, group_size, AB, BB * BB),
        pair_blocks.reshape(turn_count, group_size, 3),
        partners.reshape(turn_count, group_size, NNB),
        partner_blocks.reshape(turn_count, group_size, NNB, 3),
    )

    def group_terms(chi_acc, pieces):
        own_blocks, own_ids, slot_ids, far_ids = pieces
        blocks_split = received[slot_ids.reshape(-1)].reshape(group_size, NNB, AB, BB, BB)
        occ_tiles = occ_grid[own_ids[:, 0][:, None] - first_block, slot_ids]
        vir_tiles = vir_grid[own_ids[:, 1][:, None] - first_block, slot_ids]
        mixed_occ = jnp.einsum(
            "gtml,gtqls->gtqms", occ_tiles, blocks_split, preferred_element_type=jnp.float32
        ).astype(jnp.bfloat16)
        paired = jnp.einsum(
            "gtns,gtqms->gtqmn", vir_tiles, mixed_occ, preferred_element_type=jnp.float32
        ).astype(jnp.bfloat16)
        chi_tiles = jnp.einsum(
            "gpk,gtqk->gtpq",
            own_blocks,
            paired.reshape(group_size, NNB, AB, BB * BB),
            preferred_element_type=jnp.float32,
        )
        far_hot = (far_ids[:, :, 2][:, :, None] == jnp.arange(NAB, dtype=jnp.int32)).astype(
            jnp.float32
        )
        tile_rows = jnp.einsum("gtpq,gtb->gpbq", chi_tiles, far_hot).reshape(
            group_size, AB, aux_total
        )
        for member in range(group_size):
            target = own_ids[member, 2]
            current = lax.dynamic_slice_in_dim(chi_acc, target, 1, 0)
            chi_acc = lax.dynamic_update_slice_in_dim(
                chi_acc, current + tile_rows[member][None], target, 0
            )
        return (chi_acc, None)

    start_value = jnp.zeros((NAB, AB, aux_total), jnp.float32)
    chi_acc, unused = lax.scan(group_terms, start_value, inputs)
    chi_partial = chi_acc.reshape(aux_total, aux_total)
    share_rows = aux_total // row_count
    share_cols = aux_total // col_count
    ordered = chi_partial.reshape(row_count, share_rows, col_count, share_cols).transpose(
        0, 2, 1, 3
    )
    ordered = ordered.reshape(row_count * col_count * share_rows, share_cols)
    return lax.psum_scatter(ordered, ("row", "col"), scatter_dimension=0, tiled=True)


def solution(mesh):
    return jax.shard_map(
        body,
        mesh=mesh,
        in_specs=(
            P(("row", "col"), None),
            P(("row", "col"), None),
            P(),
            P(),
            P(("row", "col"), None, None),
            P(("row", "col"), None),
            P(("row", "col"), None),
            P(("row", "col"), None),
            P(("row", "col"), None, None),
        ),
        out_specs=P("row", "col"),
        check_vma=False,
    )
```

profile of v0, /device:TPU:32, one launch (start us, length us, event | category | flops | bytes accessed | tf_op | source)
XLA Modules:
  0.0 1998.1 jit_solution(8231398049418851729)
XLA Ops:
  6.5 0.7 fusion.29
  7.2 0.8 copy.79
  8.0 0.6 gather_fusion.4
  8.8 3.9 gather_fusion.5
  12.7 8.8 all-to-all-start.1
  21.5 5.7 gather_fusion.6
  27.3 85.5 %all-to-all-done.1 = bf16[32,16,4096]{2,1,0:T(8,128)(2,1)} async-done(((bf16[32,16,4096]{2,1,0:T(8,128)(2,1)}), bf16[32,16,4096]{2,1,0:T(8,128)(2,1)}, u32[]{:S(2)}, u32[]{:S(2)}) %all-to-all-start.1) | async-done | bytes 4194336 | tf_op jit(solution)/shard_map/all_to_all | solution.py:39
  112.7 8.6 all-to-all-start.2
  121.4 3.1 gather_fusion.3
  124.5 225.6 %all-to-all-done.2 = bf16[32,16,10240]{2,1,0:T(8,128)(2,1)} async-done(((bf16[32,16,10240]{2,1,0:T(8,128)(2,1)}), bf16[32,16,10240]{2,1,0:T(8,128)(2,1)}, u32[]{:S(2)}, u32[]{:S(2)}) %all-to-all-start.2) | async-done | bytes 10485792 | tf_op jit(solution)/shard_map/all_to_all | solution.py:40
  350.0 8.2 all-to-all-start
  358.4 3.6 convolution_convert_fusion
  362.0 0.6 reshape.118
  362.6 1.2 copy.69
  363.8 7.9 fusion.27
  371.8 0.6 reshape.121
  372.4 1.2 copy.70
  373.6 31.3 %all-to-all-done = bf16[32,128,256]{2,1,0:T(8,128)(2,1)S(1)} async-done(((bf16[32,128,256]{2,1,0:T(8,128)(2,1)}), bf16[32,128,256]{2,1,0:T(8,128)(2,1)S(1)}, u32[]{:S(2)}, u32[]{:S(2)}) %all-to-all-start) | async-done | bytes 2097184 | tf_op jit(solution)/shard_map/all_to_all | solution.py:38
  404.9 1.1 broadcast_in_dim.6
  406.0 73.5 %while.10 = (s32[]{:T(128)}, f32[4,128,512]{2,1,0:T(8,128)}, s32[2,4,3]{2,1,0:T(4,128)S(1)}, s32[2,4,12,3]{2,1,0,3:T(4,128)S(1)}, s32[2,4,12]{2,1,0:T(4,128)S(1)...) while((s32[]{:T(128)}, f32[4,128,512]{2,1,0:T(8,128)}, ...), condition=%wide.region_1.2_spmd, body=%wide.region_0.1_spmd.sunk | while | flops 513017792 | bytes 68577648 | solution.py:99
  406.0 0.2 fusion.65
  406.3 0.1 reshape.209
  406.4 1.0 copy-done
  407.4 2.3 gather_fusion.2
  409.7 2.8 copy.97
  412.5 0.1 reshape.208
  412.6 2.0 gather_fusion.1
  414.6 2.8 convert_bitcast_fusion.2
  417.6 0.1 reshape.207
  417.7 2.0 gather_fusion
  419.7 1.0 fusion.67
  420.7 3.4 convolution_bitcast_fusion.4
  424.1 3.3 copy.98
  427.5 0.4 convolution_bitcast_fusion.5
  427.9 1.0 fusion.68
  428.9 1.2 slice.113
  430.1 0.7 fusion.64
  432.9 1.1 slice.114
  435.7 1.1 slice.115
  438.7 1.1 slice.116
  441.8 1.0 copy-done.4
  442.8 0.2 fusion.65
  443.0 0.1 reshape.209
  443.1 1.0 copy-done
  444.1 2.3 gather_fusion.2
  446.5 2.8 copy.97
  449.4 2.0 gather_fusion.1
  451.4 2.8 convert_bitcast_fusion.2
  454.3 0.1 reshape.207
  454.4 2.0 gather_fusion
  456.5 1.0 fusion.67
  457.4 3.4 convolution_bitcast_fusion.4
  460.9 3.3 copy.98
  464.2 0.4 convolution_bitcast_fusion.5
  464.7 1.0 fusion.68
  465.7 1.2 slice.113
  466.9 0.7 fusion.64
  469.7 1.1 slice.114
  472.5 1.1 slice.115
  475.5 1.1 slice.116
  478.5 1.0 copy-done.4
  479.5 1.6 reshape_reshape.3
  481.1 1.7 copy.71
  482.9 1508.4 %reduce-scatter.2.cloned.1.call-done = f32[16,64]{1,0:T(8,128)} async-done(((f32[4096,64]{1,0:T(8,128)}), f32[16,64]{1,0:T(8,128)}) %reduce-scatter.2.cloned.1.call-update) | async-done | bytes 4112 | tf_op jit(solution)/shard_map/reduce_scatter | solution.py:107
  (56 shorter events, 1.2 us)
Async XLA Ops:
  12.7 8.8 copy-start.2
  12.7 100.0 %all-to-all-start.1 = ((bf16[32,16,4096]{2,1,0:T(8,128)(2,1)}), bf16[32,16,4096]{2,1,0:T(8,128)(2,1)}, u32[]{:S(2)}, u32[]{:S(2)}) async-start(bf16[32,16,4096]{2,1,0:T(8,128)(2,1)} %gather_fusion.5), calls=%async_computation.1 | async-start | bytes 8388608 | tf_op jit(solution)/shard_map/all_to_all | solution.py:39
  112.7 237.3 %all-to-all-start.2 = ((bf16[32,16,10240]{2,1,0:T(8,128)(2,1)}), bf16[32,16,10240]{2,1,0:T(8,128)(2,1)}, u32[]{:S(2)}, u32[]{:S(2)}) async-start(bf16[32,16,10240]{2,1,0:T(8,128)(2,1)} %gather_fusion.6), calls=%async_computation.2 | async-start | bytes 20971520 | tf_op jit(solution)/shard_map/all_to_all | solution.py:40
  124.5 233.9 %copy-start.5 = (bf16[96,4096]{1,0:T(8,128)(2,1)S(1)}, bf16[96,4096]{1,0:T(8,128)(2,1)}, u32[]{:S(2)}) copy-start(bf16[96,4096]{1,0:T(8,128)(2,1)} %param.11) | copy-start | bytes 2359300
  124.5 233.9 %copy-start.9 = (f32[4096]{0:T(1024)S(1)}, f32[4096]{0:T(1024)}, u32[]{:S(2)}) copy-start(f32[4096]{0:T(1024)} %param.13) | copy-start | bytes 49156
  350.0 54.8 %all-to-all-start = ((bf16[32,128,256]{2,1,0:T(8,128)(2,1)}), bf16[32,128,256]{2,1,0:T(8,128)(2,1)S(1)}, u32[]{:S(2)}, u32[]{:S(2)}) async-start(bf16[32,128,256]{2,1,0:T(8,128)(2,1)} %gather_fusion.3), calls=%async_computation | async-start | bytes 4194304 | tf_op jit(solution)/shard_map/all_to_all | solution.py:38
  358.3 1633.0 %reduce-scatter.2.cloned.1.call-start = ((), (), s32[]{:S(2)}) async-start(), calls=%async_computation.4 | async-start | bytes 2105344 | tf_op jit(solution)/shard_map/reduce_scatter | solution.py:107
  358.3 5.5 copy-start.7
  371.7 34.3 %copy-start.6 = (s32[8,12,3]{1,0,2:T(8,128)S(1)}, s32[8,12,3]{1,0,2:T(8,128)}, u32[]{:S(2)}) copy-start(s32[8,12,3]{1,0,2:T(8,128)} %param.19) | copy-start | bytes 3460
  371.7 34.3 %copy-start.8 = (s32[8,12]{1,0:T(8,128)S(1)}, s32[8,12]{1,0:T(8,128)}, u32[]{:S(2)}) copy-start(s32[8,12]{1,0:T(8,128)} %param.18) | copy-start | bytes 1156
  406.0 1.4 copy-start
  427.4 5.4 copy-start.3
  428.9 13.9 copy-start.1
  441.8 1.0 copy-start.4
  442.8 1.4 copy-start
  464.2 5.4 copy-start.3
  465.7 13.9 copy-start.1
  478.5 1.0 copy-start.4
Sparse Core Ops, SparseCore 0:
  483.0 1508.2 reduce-scatter.1
where the time goes:
time: 2000 us
  waiting for transfers between devices  1850 us (92%)
  local copies, waits for them, and re-layouts  64.1 us (3%)
  matrix products  26.9 us (1%)
  starting transfers between devices  25.7 us (1%)
    reduce_scatter x1, waiting for transfers between devices, body(): lax.psum_scatter(ordered, ('row', 'col'), scatter_dimension=0, tiled=True)  1510 us
    all_to_all x1, waiting for transfers between devices, body(): lax.all_to_all(out_vir, 'row', split_axis=0, concat_axis=0, tiled=True)  226 us
    all_to_all x1, waiting for transfers between devices, body(): lax.all_to_all(out_occ, 'row', split_axis=0, concat_axis=0, tiled=True)  85.5 us
  transfers between devices with their start and end apart: 4, of which 4 were waited for; matrix products, arithmetic and copies ran while one was open for 1% of the time, Pallas kernels for 0%

commit v1 on v0

v1 whole, which is shorter than its diff:
```python
import functools

import jax
import jax.numpy as jnp
from jax import lax
from jax.experimental import pallas as pl
from jax.experimental.pallas import tpu as pltpu
from jax.sharding import Mesh, PartitionSpec as P

BB = 16
AB = 128
NNB = 12
NAB = 4
NJ = 8
NZ = 4
NX = 4
NS = NZ * NX
LOCAL = 6
KO = 256
KV = 640
KS = KO + KV
ROWS = LOCAL * BB
TR = NNB * BB
ALL = ("zl", "x", "c", "y", "zh")
f32 = jnp.float32
bf16 = jnp.bfloat16


def dens_kernel(tab, pos, mine, other, wts, out0, out1, out2, out3, own, far, prod):
    zl, x, c = pos[0], pos[1], pos[2]
    lane = lax.broadcasted_iota(jnp.int32, (BB, NJ * BB), 1) // BB
    w_occ = wts[0:1, 0:KO]
    w_vir = wts[0:1, KO:KS]
    for k, out in enumerate((out0, out1, out2, out3)):

        def per_dest(m, carry, k=k, out=out):
            d = ((zl + m) % NZ) * NX + (x + k) % NX
            at_row = m * NX + k
            for j in range(NJ):
                a = pl.multiple_of(tab[at_row, 64 + j] * BB, BB)
                b = pl.multiple_of(tab[at_row, 72 + j] * BB, BB)
                rows = slice(j * BB, (j + 1) * BB)
                own[rows, 0:KO] = (mine[d, pl.ds(a, BB), 0:KO].astype(f32) * w_occ).astype(bf16)
                own[rows, KO:KS] = (mine[d, pl.ds(b, BB), KO:KS].astype(f32) * w_vir).astype(bf16)
            for p in range(NS):
                for q, src in enumerate((mine, other)):
                    e = 2 * p + (c ^ q)
                    a = pl.multiple_of(tab[at_row, e] * BB, BB)
                    b = pl.multiple_of(tab[at_row, 32 + e] * BB, BB)
                    to = pl.ds(pl.multiple_of(e * BB, BB), BB)
                    far[to, 0:KO] = src[p, pl.ds(a, BB), 0:KO]
                    far[to, KO:KS] = src[p, pl.ds(b, BB), KO:KS]
            dims = (((1,), (1,)), ((), ()))
            prod[0] = lax.dot_general(far[:, 0:KO], own[:, 0:KO], dims, preferred_element_type=f32)
            prod[1] = lax.dot_general(far[:, KO:KS], own[:, KO:KS], dims, preferred_element_type=f32)
            for t in range(NNB):
                parts = [None, None]
                for j in range(NJ):
                    at = pl.multiple_of(tab[at_row, 128 + j * NNB + t] * BB, BB)
                    for kind in range(2):
                        row = prod[kind, pl.ds(at, BB), :]
                        parts[kind] = row if j == 0 else jnp.where(lane == j, row, parts[kind])
                for kind in range(2):
                    out[m, kind * TR + t * BB : kind * TR + (t + 1) * BB, :] = parts[kind].astype(bf16)
            return carry

        lax.fori_loop(0, NZ, per_dest, 0)


def tile_kernel(meta, t0, t1, t2, t3, recv, own, out, dens, occ_exp, vir_exp, kron, acc, chi):
    total = t0[...].astype(f32) + t1[...].astype(f32) + t2[...].astype(f32) + t3[...].astype(f32)
    dens[...] = total.astype(bf16)
    chi[...] = jnp.zeros_like(chi)
    row = lax.broadcasted_iota(jnp.int32, (NJ * BB, BB * BB), 0)
    col = lax.broadcasted_iota(jnp.int32, (NJ * BB, BB * BB), 1)

    def per_pair(j, carry):
        hot_occ = (row == j * BB + col // BB).astype(f32).astype(bf16)
        hot_vir = (row == j * BB + col % BB).astype(f32).astype(bf16)
        occ_exp[...] = jnp.dot(dens[0:TR, :], hot_occ, preferred_element_type=f32)
        vir_exp[...] = jnp.dot(dens[TR : 2 * TR, :], hot_vir, preferred_element_type=f32)
        acc[...] = jnp.zeros_like(acc)
        for t in range(NNB):
            buf = t % 2
            vir = vir_exp[t * BB : (t + 1) * BB, :]
            for lam in range(BB):
                occ = jnp.broadcast_to(occ_exp[t * BB + lam : t * BB + lam + 1, :], (BB, BB * BB))
                kron[buf, lam * BB : (lam + 1) * BB, :] = (occ * vir).astype(bf16)
            slot = meta[j * NNB + t]
            aux = meta[128 + j * NNB + t]
            paired = jnp.dot(recv[slot], kron[buf], preferred_element_type=f32)
            acc[aux] = acc[aux] + paired
        target = meta[240 + j]
        rows = acc[...].reshape(NAB * AB, BB * BB).astype(bf16)
        chi[target] += lax.dot_general(
            own[j], rows, (((1,), (1,)), ((), ())), preferred_element_type=f32
        )
        return carry

    lax.fori_loop(0, NJ, per_pair, 0)
    low = lax.broadcasted_iota(jnp.int32, (1, 8, 128), 2) < 64
    for tile in range(4):
        grid = chi[:, :, tile * 128 : (tile + 1) * 128].reshape(32, 2, 8, 128)
        top, bot = grid[:, 0], grid[:, 1]
        even = jnp.where(low, top, pltpu.roll(bot, 64, 2))
        odd = jnp.where(low, pltpu.roll(top, 64, 2), bot)
        out[:, 2 * tile] = even.astype(bf16)
        out[:, 2 * tile + 1] = odd.astype(bf16)


def around(rows, axis, size):
    parts = [rows]
    for k in range(1, size):
        parts.append(lax.ppermute(rows, axis, [((i + k) % size, i) for i in range(size)]))
    return jnp.concatenate(parts, axis=0)


def body(
    occ_coef,
    vir_coef,
    occ_weight,
    vir_weight,
    three_center,
    pair_blocks,
    send_pairs,
    partners,
    partner_blocks,
):
    zl, x, c = lax.axis_index("zl"), lax.axis_index("x"), lax.axis_index("c")
    share = zl * NX + x
    payload = jnp.concatenate(
        [
            occ_coef.reshape(ROWS, NS, KO).transpose(1, 0, 2),
            vir_coef.reshape(ROWS, NS, KV).transpose(1, 0, 2),
        ],
        axis=2,
    )
    mine = lax.all_to_all(payload, ("zl", "x"), split_axis=0, concat_axis=0, tiled=True)

    wts = jnp.concatenate(
        [
            lax.dynamic_slice_in_dim(occ_weight, share * KO, KO),
            lax.dynamic_slice_in_dim(vir_weight, share * KV, KV),
        ]
    ).reshape(1, KS)
    slots = partners.reshape(-1)
    far_ids = partner_blocks.reshape(-1, 3)
    own_local = pair_blocks % LOCAL
    far_local = far_ids % LOCAL
    hot = slots[:, None] == jnp.arange(32, dtype=jnp.int32)[None, :]
    slot_occ = jnp.max(jnp.where(hot, far_local[:, 0:1], 0), axis=0)
    slot_vir = jnp.max(jnp.where(hot, far_local[:, 1:2], 0), axis=0)
    pad = jnp.zeros((48,), jnp.int32)
    table = jnp.concatenate(
        [slot_occ, slot_vir, own_local[:, 0], own_local[:, 1], pad, slots, pad[:32]]
    )
    tables = around(around(table.reshape(1, 256), "x", NX), "zl", NZ)
    pos = jnp.stack([zl, x, c, share]).astype(jnp.int32)
    out_blocks = three_center[send_pairs.reshape(-1)]

    mine, out_blocks, tables, wts = lax.optimization_barrier((mine, out_blocks, tables, wts))
    received = lax.all_to_all(
        out_blocks, ("zl", "x", "c"), split_axis=0, concat_axis=0, tiled=True
    )
    other = lax.ppermute(mine, "c", [(0, 1), (1, 0)])

    vmem = pl.BlockSpec(memory_space=pltpu.VMEM)
    smem = pl.BlockSpec(memory_space=pltpu.SMEM)
    part = jax.ShapeDtypeStruct((NZ, 2 * TR, NJ * BB), bf16)
    partials = pl.pallas_call(
        dens_kernel,
        out_shape=(part,) * NX,
        in_specs=[smem, smem, vmem, vmem, vmem],
        out_specs=(vmem,) * NX,
        scratch_shapes=[
            pltpu.VMEM((NJ * BB, KS), bf16),
            pltpu.VMEM((32 * BB, KS), bf16),
            pltpu.VMEM((2, 32 * BB, NJ * BB), f32),
        ],
        compiler_params=pltpu.CompilerParams(vmem_limit_bytes=32 << 20),
        cost_estimate=pl.CostEstimate(
            flops=2 * NS * 512 * 128 * KS, bytes_accessed=8 << 20, transcendentals=0
        ),
        name="density_partials",
    )(tables, pos, mine, other, wts)
    summed = partials[0].astype(f32)
    for k in range(1, NX):
        moved = lax.ppermute(partials[k], "x", [(i, (i + k) % NX) for i in range(NX)])
        summed = summed + moved.astype(f32)
    tiles = [summed[0].astype(bf16)]
    for m in range(1, NZ):
        tiles.append(
            lax.ppermute(summed[m].astype(bf16), "zl", [(i, (i + m) % NZ) for i in range(NZ)])
        )

    pad32 = pad[:32]
    meta = jnp.concatenate([slots, pad32, far_ids[:, 2], pad[:16], pair_blocks[:, 2], pad[:8]])
    packed = pl.pallas_call(
        tile_kernel,
        out_shape=jax.ShapeDtypeStruct((32, 8, 8, 128), bf16),
        in_specs=[smem] + [vmem] * 6,
        out_specs=vmem,
        scratch_shapes=[
            pltpu.VMEM((2 * TR, NJ * BB), bf16),
            pltpu.VMEM((TR, BB * BB), f32),
            pltpu.VMEM((TR, BB * BB), f32),
            pltpu.VMEM((2, BB * BB, BB * BB), bf16),
            pltpu.VMEM((NAB, AB, BB * BB), f32),
            pltpu.VMEM((NAB, AB, NAB * AB), f32),
        ],
        compiler_params=pltpu.CompilerParams(vmem_limit_bytes=32 << 20),
        cost_estimate=pl.CostEstimate(
            flops=2 * 96 * 128 * 256 * 256, bytes_accessed=4 << 20, transcendentals=0
        ),
        name="chi_tiles",
    )(meta, *tiles, received, three_center)

    gathered = lax.all_to_all(
        packed.reshape(256, 8, 128), ALL, split_axis=0, concat_axis=0, tiled=True
    )
    total = jnp.sum(gathered.astype(f32), axis=0)
    return jnp.concatenate([total[:, :64], total[:, 64:]], axis=0)


def solution(mesh):
    fine = Mesh(mesh.devices.reshape(4, 4, 2, 4, 2), ALL)
    return jax.shard_map(
        body,
        mesh=fine,
        in_specs=(
            P(ALL, None),
            P(ALL, None),
            P(),
            P(),
            P(ALL, None, None),
            P(ALL, None),
            P(ALL, None),
            P(ALL, None),
            P(ALL, None, None),
        ),
        out_specs=P(("zl", "x", "c"), ("y", "zh")),
        check_vma=False,
    )
```

time: 2000 us -> 187 us (0.09)
  waiting for transfers between devices: 1850 us -> 79.4 us
  local copies, waits for them, and re-layouts: 64.1 us -> 7.01 us
  blocking collectives: 0 us -> 32.3 us
  matrix products: 26.9 us -> 0 us
  Pallas kernels: 0 us -> 22.8 us
    reduce_scatter x1 -> x0, waiting for transfers between devices: 1510 us -> none  [body(): lax.psum_scatter(ordered, ('row', 'col'), scatter_dimension=0, tiled=True)]
    all_to_all x3 -> x2, waiting for transfers between devices: 342 us -> 0.01 us  [the longest x1 0.01 us: body(): lax.all_to_all(payload, ('zl', 'x'), split_axis=0, concat_axis=0, tiled=T...]
    ppermute x0 -> x13, waiting for transfers between devices: none -> 79.4 us  [the longest x6 43.3 us: around(): lax.ppermute(rows, axis, [((i + k) % size, i) for i in range(size)])]
    all_to_all x0 -> x1, blocking collectives: none -> 32.3 us  [body(): lax.all_to_all(packed.reshape(256, 8, 128), ALL, split_axis=0, concat_axi...]
    gather x12 -> x1, local copies, waits for them, and re-layouts: 31.8 us -> 2.04 us  [body(): out_blocks = three_center[send_pairs.reshape(-1)]]
    dot_general x10 -> x0, matrix products: 26.9 us -> none  [the longest x1 7.93 us: body(): jnp.einsum('mi,li->ml', scaled_vir, recv_vir.reshape(slot_total * BB, vir...]
    ppermute x0 -> x13, starting transfers between devices: none -> 23.7 us  [the longest x6 13.9 us: around(): lax.ppermute(rows, axis, [((i + k) % size, i) for i in range(size)])]
    pallas_call x0 -> x2, Pallas kernels: none -> 22.8 us  [the longest x1 14 us: body(): pl.pallas_call(dens_kernel, out_shape=(part,) * NX, in_specs=[smem, smem,...]
  transfers between devices with their start and end apart: 4 -> 15, of which waited for: 4 -> 10; matrix products, arithmetic and copies ran while one was open for 1% -> 2% of each run, Pallas kernels for 0% -> 8%
where the time goes in v1:
time: 187 us; the launch traced here: 184 us
  waiting for transfers between devices  79.4 us (42%)
  starting transfers between devices  39.1 us (21%)
  blocking collectives  32.3 us (17%)
  Pallas kernels  22.8 us (12%)
  local copies, waits for them, and re-layouts  7.01 us (4%)
  other arithmetic  3.11 us (2%)
    ppermute x6, waiting for transfers between devices, around(): lax.ppermute(rows, axis, [((i + k) % size, i) for i in range(size)])  43.3 us
    all_to_all x1, blocking collectives, body(): lax.all_to_all(packed.reshape(256, 8, 128), ALL, split_axis=0, concat_axi...  32.3 us
    ppermute x3, waiting for transfers between devices, body(): lax.ppermute(partials[k], 'x', [(i, (i + k) % NX) for i in range(NX)])  24.9 us
    pallas_call x1, Pallas kernels, body(): pl.pallas_call(dens_kernel, out_shape=(part,) * NX, in_specs=[smem, smem,...  14 us
    ppermute x6, starting transfers between devices, around(): lax.ppermute(rows, axis, [((i + k) % size, i) for i in range(size)])  13.9 us
    pallas_call x1, Pallas kernels, body(): pl.pallas_call(tile_kernel, out_shape=jax.ShapeDtypeStruct((32, 8, 8, 128...  8.8 us
    all_to_all x1, starting transfers between devices, body(): lax.all_to_all(payload, ('zl', 'x'), split_axis=0, concat_axis=0, tiled=T...  8.63 us
    all_to_all x1, starting transfers between devices, body(): lax.all_to_all(out_blocks, ('zl', 'x', 'c'), split_axis=0, concat_axis=0,...  6.78 us
  transfers between devices with their start and end apart: 15, of which 10 were waited for; matrix products, arithmetic and copies ran while one was open for 2% of the time, Pallas kernels for 8%

profile of v1, /device:TPU:32, one launch (start us, length us, event | category | flops | bytes accessed | tf_op | source)
XLA Modules:
  0.0 183.9 jit_solution(4884044962695906614)
XLA Ops:
  0.0 1.2 copy.19
  1.2 1.7 copy.18
  2.9 1.8 pad_maximum_fusion
  4.7 0.0 copy-start.2
  4.7 0.0 copy-start.1
  4.7 0.0 copy-start.3
  4.7 0.0 copy-start.4
  4.7 0.0 copy-start
  4.7 8.6 %all-to-all-start = ((bf16[16,96,896]{2,1,0:T(8,128)(2,1)}), bf16[16,96,896]{2,1,0:T(8,128)(2,1)S(1)}, u32[]{:S(2)}, u32[]{:S(2)}) async-start(bf16[16,96,896]{2,1,0:T(8,128)(2,1)} %pad_maximum_fusion), calls=%async_computation | async-start | bytes 5505024 | tf_op jit(solution)/shard_map/all_to_all | solution.py:138
  13.4 0.0 copy-done.2
  13.4 0.1 reshape.27
  13.4 0.0 copy-done.1
  13.4 0.1 reshape.28
  13.6 0.1 select_reduce_fusion
  13.7 0.0 copy-done.3
  13.7 0.1 concatenate.24
  13.8 1.5 collective-permute-start.2
  15.3 2.7 %collective-permute-start.1 = (s32[1,256]{1,0:T(1,128)S(1)}, s32[1,256]{1,0:T(1,128)S(1)}, u32[]{:S(2)}, u32[]{:S(2)}) collective-permute-start(s32[1,256]{1,0:T(1,128)S(1)} %bitcast.50), channel_id=1, source_target_pairs={{32,0},{48,16},{0,32},{16,48},{33,1},{49,17},{1,33},{17,49},{34,2}... | collective-permute-start | bytes 3080 | tf_op jit(solution)/shard_map/ppermute | solution.py:114
  18.0 1.5 collective-permute-start
  19.4 0.0 copy-done.4
  19.5 0.8 dynamic_slice.6
  20.2 0.8 dynamic_slice.7
  21.0 6.5 %collective-permute-done.2 = s32[1,256]{1,0:T(1,128)S(1)} collective-permute-done((s32[1,256]{1,0:T(1,128)S(1)}, s32[1,256]{1,0:T(1,128)S(1)}, u32[]{:S(2)}, u32[]{:S(2)}) %collective-permute-start.2) | collective-permute-done | bytes 1056 | tf_op jit(solution)/shard_map/ppermute | solution.py:114
  27.5 0.3 collective-permute-done.1
  27.8 0.0 collective-permute-done
  27.8 1.8 collective-permute-start.5
  29.6 4.6 %collective-permute-start.4 = (s32[4,256]{1,0:T(4,128)S(1)}, s32[4,256]{1,0:T(4,128)S(1)}, u32[]{:S(2)}, u32[]{:S(2)}) collective-permute-start(s32[4,256]{1,0:T(4,128)S(1)} %pad_add_fusion), channel_id=1, source_target_pairs={{128,0},{192,64},{0,128},{64,192},{129,1},{193,65},{1,129},{65,193... | collective-permute-start | bytes 12296 | tf_op jit(solution)/shard_map/ppermute | solution.py:114
  34.1 1.9 %collective-permute-start.3 = (s32[4,256]{1,0:T(4,128)S(1)}, s32[4,256]{1,0:T(4,128)S(1)}, u32[]{:S(2)}, u32[]{:S(2)}) collective-permute-start(s32[4,256]{1,0:T(4,128)S(1)} %pad_add_fusion), channel_id=1, source_target_pairs={{64,0},{128,64},{192,128},{0,192},{65,1},{129,65},{193,129},{1,193... | collective-permute-start | bytes 12296 | tf_op jit(solution)/shard_map/ppermute | solution.py:114
  36.1 0.0 copy-done
  36.1 2.0 %gather_fusion = bf16[32,128,256]{2,1,0:T(8,128)(2,1)} fusion(bf16[8,128,256]{2,1,0:T(8,128)(2,1)S(1)} %copy-done, s32[1024]{0:T(1024)S(1)} %pad_clamp_fusion), kind=kCustom, calls=%fused_computation | custom fusion | bytes 4194432 | tf_op jit(solution)/shard_map/gather | solution.py:159
  38.1 34.5 %collective-permute-done.5 = s32[4,256]{1,0:T(4,128)S(1)} collective-permute-done((s32[4,256]{1,0:T(4,128)S(1)}, s32[4,256]{1,0:T(4,128)S(1)}, u32[]{:S(2)}, u32[]{:S(2)}) %collective-permute-start.5) | collective-permute-done | bytes 4128 | tf_op jit(solution)/shard_map/ppermute | solution.py:114
  72.6 0.0 collective-permute-done.4
  72.6 1.9 %collective-permute-done.3 = s32[4,256]{1,0:T(4,128)S(1)} collective-permute-done((s32[4,256]{1,0:T(4,128)S(1)}, s32[4,256]{1,0:T(4,128)S(1)}, u32[]{:S(2)}, u32[]{:S(2)}) %collective-permute-start.3) | collective-permute-done | bytes 4128 | tf_op jit(solution)/shard_map/ppermute | solution.py:114
  74.6 0.0 all-to-all-done.mine
  74.6 6.8 %all-to-all-start.1 = ((bf16[32,128,256]{2,1,0:T(8,128)(2,1)}), bf16[32,128,256]{2,1,0:T(8,128)(2,1)}, u32[]{:S(2)}, u32[]{:S(2)}) async-start(bf16[32,128,256]{2,1,0:T(8,128)(2,1)} %gather_fusion), calls=%async_computation.1 | async-start | bytes 4194304 | tf_op jit(solution)/shard_map/all_to_all | solution.py:162
  81.4 0.2 collective-permute-start.6
  81.7 0.1 pad_add_fusion.1.pos
  81.7 5.0 %collective-permute-done.6.other = bf16[16,96,896]{2,1,0:T(8,128)(2,1)} collective-permute-done((bf16[16,96,896]{2,1,0:T(8,128)(2,1)S(1)}, bf16[16,96,896]{2,1,0:T(8,128)(2,1)}, u32[]{:S(2)}, u32[]{:S(2)}) %collective-permute-start.6) | collective-permute-done | bytes 2752544 | tf_op jit(solution)/shard_map/ppermute | solution.py:165
  86.7 14.0 %density_partials.1 = (bf16[4,384,128]{2,1,0:T(8,128)(2,1)S(1)}, bf16[4,384,128]{2,1,0:T(8,128)(2,1)S(1)}, bf16[4,384,128]{2,1,0:T(8,128)(2,1)S(1)}, bf16[4,384,128]{2,1,0:T(8,128)(2,1)S(1)}) custom-call(s32[16,256]{1,0:T(8,128)S(1)} %concatenate.26.tab, s32[4]{0:T(128)S(1)} %pad_add_fusion.1.pos, bf16[16,96,896]{2,1,0:T(8,128)(2,1)S(1)} %all-to-all-done.mine, ...), custom_call_target="tpu_custom_call" | custom-call | flops 1879048192 | bytes 8388608 | tf_op jit(solution)/shard_map/density_partials/pallas_call | solution.py:170
  100.7 1.5 collective-permute-start.7
  102.3 2.7 %collective-permute-start.8 = (bf16[4,384,128]{2,1,0:T(8,128)(2,1)S(1)}, bf16[4,384,128]{2,1,0:T(8,128)(2,1)S(1)}, u32[]{:S(2)}, u32[]{:S(2)}) collective-permute-start(bf16[4,384,128]{2,1,0:T(8,128)(2,1)S(1)} %get-tuple-element.18), channel_id=1, source_target_pairs={{0,32},{16,48},{32,0},{48,16},{1,33},{17,49},{33,1},{49,17},{2,34}... | collective-permute-start | bytes 1179656 | tf_op jit(solution)/shard_map/ppermute | solution.py:188
  104.9 1.5 collective-permute-start.9
  106.4 12.4 %collective-permute-done.7 = bf16[4,384,128]{2,1,0:T(8,128)(2,1)S(1)} collective-permute-done((bf16[4,384,128]{2,1,0:T(8,128)(2,1)S(1)}, bf16[4,384,128]{2,1,0:T(8,128)(2,1)S(1)}, u32[]{:S(2)}, u32[]{:S(2)}) %collective-permute-start.7) | collective-permute-done | bytes 393248 | tf_op jit(solution)/shard_map/ppermute | solution.py:188
  118.8 12.5 %collective-permute-done.8 = bf16[4,384,128]{2,1,0:T(8,128)(2,1)S(1)} collective-permute-done((bf16[4,384,128]{2,1,0:T(8,128)(2,1)S(1)}, bf16[4,384,128]{2,1,0:T(8,128)(2,1)S(1)}, u32[]{:S(2)}, u32[]{:S(2)}) %collective-permute-start.8) | collective-permute-done | bytes 393248 | tf_op jit(solution)/shard_map/ppermute | solution.py:188
  131.3 0.0 collective-permute-done.9
  131.3 0.2 add_convert_fusion
  131.6 0.3 collective-permute-start.12
  131.9 3.2 %collective-permute-start.11 = (bf16[384,128]{1,0:T(8,128)(2,1)S(1)}, bf16[384,128]{1,0:T(8,128)(2,1)S(1)}, u32[]{:S(2)}, u32[]{:S(2)}) collective-permute-start(bf16[384,128]{1,0:T(8,128)(2,1)S(1)} %get-tuple-element.24), channel_id=1, source_target_pairs={{0,128},{64,192},{128,0},{192,64},{1,129},{65,193},{129,1},{193,65... | collective-permute-start | bytes 294920 | tf_op jit(solution)/shard_map/ppermute | solution.py:193
  135.1 0.4 collective-permute-start.10
  135.5 0.1 concatenate.22.meta
  135.6 3.1 %collective-permute-done.12.t3 = bf16[384,128]{1,0:T(8,128)(2,1)S(1)} collective-permute-done((bf16[384,128]{1,0:T(8,128)(2,1)S(1)}, bf16[384,128]{1,0:T(8,128)(2,1)S(1)}, u32[]{:S(2)}, u32[]{:S(2)}) %collective-permute-start.12) | collective-permute-done | bytes 98336 | tf_op jit(solution)/shard_map/ppermute | solution.py:193
  138.7 1.9 %collective-permute-done.11.t2 = bf16[384,128]{1,0:T(8,128)(2,1)S(1)} collective-permute-done((bf16[384,128]{1,0:T(8,128)(2,1)S(1)}, bf16[384,128]{1,0:T(8,128)(2,1)S(1)}, u32[]{:S(2)}, u32[]{:S(2)}) %collective-permute-start.11) | collective-permute-done | bytes 98336 | tf_op jit(solution)/shard_map/ppermute | solution.py:193
  140.7 1.2 collective-permute-done.10.t1
  141.8 0.0 all-to-all-done.1.recv
  141.8 8.8 %chi_tiles.1 = bf16[32,8,8,128]{3,2,1,0:T(8,128)(2,1)S(1)} custom-call(s32[256]{0:T(256)S(1)} %concatenate.22.meta, bf16[384,128]{1,0:T(8,128)(2,1)S(1)} %get-tuple-element.26.t0, bf16[384,128]{1,0:T(8,128)(2,1)S(1)} %collective-permute-done.10.t1, bf16[384,128]{1,0:T(8,128)(2,1)S(1)} %collective-permute-done.11.t2, ...), custom_call_target="tpu_custom_call" | custom-call | flops 1610612736 | bytes 4194304 | tf_op jit(solution)/shard_map/chi_tiles/pallas_call | solution.py:198
  150.6 32.3 %all_to_all.15 = bf16[256,8,128]{2,1,0:T(8,128)(2,1)S(1)} all-to-all(bf16[256,8,128]{2,1,0:T(8,128)(2,1)S(1)} %bitcast.44), channel_id=1, replica_groups=mesh['zl'=4,'x'=4,'c'=2,'y'=4,'zh'=2] {'zl','x','c','y','zh'}, dimensions={0} | all-to-all | bytes 1048576 | tf_op jit(solution)/shard_map/all_to_all | solution.py:218
  182.9 0.3 convert_reduce_fusion
  183.2 0.1 fusion.1
  183.3 0.6 pad_maximum_fusion.1
  (17 shorter events, 0.2 us)
Async XLA Ops:
  4.7 8.7 %copy-start.2 = (s32[8,12]{1,0:T(8,128)S(1)}, s32[8,12]{1,0:T(8,128)}, u32[]{:S(2)}) copy-start(s32[8,12]{1,0:T(8,128)} %param.16) | copy-start | bytes 1156
  4.7 8.7 %copy-start.1 = (s32[8,12,3]{1,0,2:T(8,128)S(1)}, s32[8,12,3]{1,0,2:T(8,128)}, u32[]{:S(2)}) copy-start(s32[8,12,3]{1,0,2:T(8,128)} %param.17) | copy-start | bytes 3460
  4.7 9.0 %copy-start.3 = (s32[8,3]{0,1:T(4,128)S(1)}, s32[8,3]{0,1:T(4,128)}, u32[]{:S(2)}) copy-start(s32[8,3]{0,1:T(4,128)} %param.14) | copy-start | bytes 292
  4.7 14.7 %copy-start.4 = (s32[32,1]{0,1:T(1,128)S(1)}, s32[32,1]{0,1:T(1,128)}, u32[]{:S(2)}) copy-start(s32[32,1]{0,1:T(1,128)} %param.15) | copy-start | bytes 388
  4.7 31.4 %copy-start = (bf16[8,128,256]{2,1,0:T(8,128)(2,1)S(1)}, bf16[8,128,256]{2,1,0:T(8,128)(2,1)}, u32[]{:S(2)}) copy-start(bf16[8,128,256]{2,1,0:T(8,128)(2,1)} %own.1) | copy-start | bytes 1572868
  4.7 69.9 %all-to-all-start = ((bf16[16,96,896]{2,1,0:T(8,128)(2,1)}), bf16[16,96,896]{2,1,0:T(8,128)(2,1)S(1)}, u32[]{:S(2)}, u32[]{:S(2)}) async-start(bf16[16,96,896]{2,1,0:T(8,128)(2,1)} %pad_maximum_fusion), calls=%async_computation | async-start | bytes 5505024 | tf_op jit(solution)/shard_map/all_to_all | solution.py:138
  13.8 13.7 %collective-permute-start.2 = (s32[1,256]{1,0:T(1,128)S(1)}, s32[1,256]{1,0:T(1,128)S(1)}, u32[]{:S(2)}, u32[]{:S(2)}) collective-permute-start(s32[1,256]{1,0:T(1,128)S(1)} %bitcast.49), channel_id=1, source_target_pairs={{48,0},{0,16},{16,32},{32,48},{49,1},{1,17},{17,33},{33,49},{50,2}... | collective-permute-start | bytes 3080 | tf_op jit(solution)/shard_map/ppermute | solution.py:114
  15.3 12.5 %collective-permute-start.1 = (s32[1,256]{1,0:T(1,128)S(1)}, s32[1,256]{1,0:T(1,128)S(1)}, u32[]{:S(2)}, u32[]{:S(2)}) collective-permute-start(s32[1,256]{1,0:T(1,128)S(1)} %bitcast.50), channel_id=1, source_target_pairs={{32,0},{48,16},{0,32},{16,48},{33,1},{49,17},{1,33},{17,49},{34,2}... | collective-permute-start | bytes 3080 | tf_op jit(solution)/shard_map/ppermute | solution.py:114
  18.0 9.8 %collective-permute-start = (s32[1,256]{1,0:T(1,128)S(1)}, s32[1,256]{1,0:T(1,128)S(1)}, u32[]{:S(2)}, u32[]{:S(2)}) collective-permute-start(s32[1,256]{1,0:T(1,128)S(1)} %bitcast.51), channel_id=1, source_target_pairs={{16,0},{32,16},{48,32},{0,48},{17,1},{33,17},{49,33},{1,49},{18,2}... | collective-permute-start | bytes 3080 | tf_op jit(solution)/shard_map/ppermute | solution.py:114
  27.8 44.8 %collective-permute-start.5 = (s32[4,256]{1,0:T(4,128)S(1)}, s32[4,256]{1,0:T(4,128)S(1)}, u32[]{:S(2)}, u32[]{:S(2)}) collective-permute-start(s32[4,256]{1,0:T(4,128)S(1)} %pad_add_fusion), channel_id=1, source_target_pairs={{192,0},{0,64},{64,128},{128,192},{193,1},{1,65},{65,129},{129,193... | collective-permute-start | bytes 12296 | tf_op jit(solution)/shard_map/ppermute | solution.py:114
  29.6 43.0 %collective-permute-start.4 = (s32[4,256]{1,0:T(4,128)S(1)}, s32[4,256]{1,0:T(4,128)S(1)}, u32[]{:S(2)}, u32[]{:S(2)}) collective-permute-start(s32[4,256]{1,0:T(4,128)S(1)} %pad_add_fusion), channel_id=1, source_target_pairs={{128,0},{192,64},{0,128},{64,192},{129,1},{193,65},{1,129},{65,193... | collective-permute-start | bytes 12296 | tf_op jit(solution)/shard_map/ppermute | solution.py:114
  34.1 40.4 %collective-permute-start.3 = (s32[4,256]{1,0:T(4,128)S(1)}, s32[4,256]{1,0:T(4,128)S(1)}, u32[]{:S(2)}, u32[]{:S(2)}) collective-permute-start(s32[4,256]{1,0:T(4,128)S(1)} %pad_add_fusion), channel_id=1, source_target_pairs={{64,0},{128,64},{192,128},{0,192},{65,1},{129,65},{193,129},{1,193... | collective-permute-start | bytes 12296 | tf_op jit(solution)/shard_map/ppermute | solution.py:114
  74.6 67.2 %all-to-all-start.1 = ((bf16[32,128,256]{2,1,0:T(8,128)(2,1)}), bf16[32,128,256]{2,1,0:T(8,128)(2,1)}, u32[]{:S(2)}, u32[]{:S(2)}) async-start(bf16[32,128,256]{2,1,0:T(8,128)(2,1)} %gather_fusion), calls=%async_computation.1 | async-start | bytes 4194304 | tf_op jit(solution)/shard_map/all_to_all | solution.py:162
  81.4 5.3 %collective-permute-start.6 = (bf16[16,96,896]{2,1,0:T(8,128)(2,1)S(1)}, bf16[16,96,896]{2,1,0:T(8,128)(2,1)}, u32[]{:S(2)}, u32[]{:S(2)}) collective-permute-start(bf16[16,96,896]{2,1,0:T(8,128)(2,1)S(1)} %all-to-all-done.mine), channel_id=1, source_target_pairs={{0,8},{8,0},{1,9},{9,1},{2,10},{10,2},{3,11},{11,3},{4,12},{12,4},... | collective-permute-start | bytes 8257544 | tf_op jit(solution)/shard_map/ppermute | solution.py:165
  100.7 18.1 %collective-permute-start.7 = (bf16[4,384,128]{2,1,0:T(8,128)(2,1)S(1)}, bf16[4,384,128]{2,1,0:T(8,128)(2,1)S(1)}, u32[]{:S(2)}, u32[]{:S(2)}) collective-permute-start(bf16[4,384,128]{2,1,0:T(8,128)(2,1)S(1)} %get-tuple-element.17), channel_id=1, source_target_pairs={{0,16},{16,32},{32,48},{48,0},{1,17},{17,33},{33,49},{49,1},{2,18}... | collective-permute-start | bytes 1179656 | tf_op jit(solution)/shard_map/ppermute | solution.py:188
  102.3 29.1 %collective-permute-start.8 = (bf16[4,384,128]{2,1,0:T(8,128)(2,1)S(1)}, bf16[4,384,128]{2,1,0:T(8,128)(2,1)S(1)}, u32[]{:S(2)}, u32[]{:S(2)}) collective-permute-start(bf16[4,384,128]{2,1,0:T(8,128)(2,1)S(1)} %get-tuple-element.18), channel_id=1, source_target_pairs={{0,32},{16,48},{32,0},{48,16},{1,33},{17,49},{33,1},{49,17},{2,34}... | collective-permute-start | bytes 1179656 | tf_op jit(solution)/shard_map/ppermute | solution.py:188
  104.9 26.4 %collective-permute-start.9 = (bf16[4,384,128]{2,1,0:T(8,128)(2,1)S(1)}, bf16[4,384,128]{2,1,0:T(8,128)(2,1)S(1)}, u32[]{:S(2)}, u32[]{:S(2)}) collective-permute-start(bf16[4,384,128]{2,1,0:T(8,128)(2,1)S(1)} %get-tuple-element.19), channel_id=1, source_target_pairs={{0,48},{16,0},{32,16},{48,32},{1,49},{17,1},{33,17},{49,33},{2,50}... | collective-permute-start | bytes 1179656 | tf_op jit(solution)/shard_map/ppermute | solution.py:188
  131.6 7.1 %collective-permute-start.12 = (bf16[384,128]{1,0:T(8,128)(2,1)S(1)}, bf16[384,128]{1,0:T(8,128)(2,1)S(1)}, u32[]{:S(2)}, u32[]{:S(2)}) collective-permute-start(bf16[384,128]{1,0:T(8,128)(2,1)S(1)} %get-tuple-element.23), channel_id=1, source_target_pairs={{0,192},{64,0},{128,64},{192,128},{1,193},{65,1},{129,65},{193,129... | collective-permute-start | bytes 294920 | tf_op jit(solution)/shard_map/ppermute | solution.py:193
  131.9 8.8 %collective-permute-start.11 = (bf16[384,128]{1,0:T(8,128)(2,1)S(1)}, bf16[384,128]{1,0:T(8,128)(2,1)S(1)}, u32[]{:S(2)}, u32[]{:S(2)}) collective-permute-start(bf16[384,128]{1,0:T(8,128)(2,1)S(1)} %get-tuple-element.24), channel_id=1, source_target_pairs={{0,128},{64,192},{128,0},{192,64},{1,129},{65,193},{129,1},{193,65... | collective-permute-start | bytes 294920 | tf_op jit(solution)/shard_map/ppermute | solution.py:193
  135.1 6.8 %collective-permute-start.10 = (bf16[384,128]{1,0:T(8,128)(2,1)S(1)}, bf16[384,128]{1,0:T(8,128)(2,1)S(1)}, u32[]{:S(2)}, u32[]{:S(2)}) collective-permute-start(bf16[384,128]{1,0:T(8,128)(2,1)S(1)} %get-tuple-element.25), channel_id=1, source_target_pairs={{0,64},{64,128},{128,192},{192,0},{1,65},{65,129},{129,193},{193,1... | collective-permute-start | bytes 294920 | tf_op jit(solution)/shard_map/ppermute | solution.py:193

commit v2 on v1

v2 whole, which is shorter than its diff:
```python
import functools

import jax
import jax.numpy as jnp
from jax import lax
from jax.experimental import pallas as pl
from jax.experimental.pallas import tpu as pltpu
from jax.sharding import Mesh, PartitionSpec as P

BB = 16
AB = 128
NNB = 12
NAB = 4
NJ = 8
NZ = 4
NX = 4
NS = NZ * NX
LOCAL = 6
KO = 256
KV = 640
ROWS = LOCAL * BB
TR = NNB * BB
LANES = 128
TO = KO // LANES
TV = KV // LANES
KT = TO + TV
BLK = KT * BB
PAY = LOCAL * BLK + 8
ALL = ("zl", "x", "c", "y", "zh")
f32 = jnp.float32
bf16 = jnp.bfloat16


def table_of(ids, slots, far_ids):
    lane = lax.broadcasted_iota(jnp.int32, (NJ, LANES), 1)
    diag = lax.broadcasted_iota(jnp.int32, (NJ, NJ), 0) == lax.broadcasted_iota(jnp.int32, (NJ, NJ), 1)
    slot = slots[...]

    def local(block):
        return block - LOCAL * jnp.floor((block.astype(f32) + 0.5) * (1.0 / LOCAL)).astype(jnp.int32)

    own = local(ids[...])
    far_occ, far_vir = local(far_ids[0]), local(far_ids[1])
    rows = jnp.zeros((NJ, LANES), jnp.int32)
    for kind in range(2):
        column = jnp.sum(jnp.where(diag, own[kind : kind + 1, :], 0), axis=1, keepdims=True)
        rows = jnp.where(lane == 16 + kind, column, rows)
    seen = jnp.zeros((NJ, LANES), jnp.int32)
    for t in range(NNB):
        here = slot[:, t : t + 1]
        rows = jnp.where(lane == t, here, rows)
        seen = jnp.where(lane == here + 32, jnp.maximum(seen, far_occ[:, t : t + 1]), seen)
        seen = jnp.where(lane == here + 64, jnp.maximum(seen, far_vir[:, t : t + 1]), seen)
    rows = rows + jnp.max(seen, axis=0, keepdims=True)
    return rows.astype(f32).astype(bf16)


def payload_kernel(occ, vir, *refs):
    given, (out, occ_in, vir_in, packed, *small, sems_in, sems_out) = refs[:3], refs[3:]
    copies = [pltpu.make_async_copy(given[n], small[n], sems_in.at[NS, n]) for n in range(3)]
    for copy in copies:
        copy.start()
    loads, stores = [], []
    for s in range(NS):
        loads.append(
            (
                pltpu.make_async_copy(occ.at[:, pl.ds(s * KO, KO)], occ_in.at[s], sems_in.at[s, 0]),
                pltpu.make_async_copy(vir.at[:, pl.ds(s * KV, KV)], vir_in.at[s], sems_in.at[s, 1]),
            )
        )
        for load in loads[-1]:
            load.start()
    for copy in copies:
        copy.wait()
    table = table_of(*small)
    for s in range(NS):
        for load in loads[s]:
            load.wait()
        for blk in range(LOCAL):
            rows = slice(blk * BB, (blk + 1) * BB)
            for kt in range(KT):
                at = blk * BLK + kt * BB
                stage, first = (occ_in, kt) if kt < TO else (vir_in, kt - TO)
                packed[s, at : at + BB, :] = stage[s, rows, first * LANES : (first + 1) * LANES]
        packed[s, LOCAL * BLK : PAY, :] = table
        stores.append(pltpu.make_async_copy(packed.at[s], out.at[s], sems_out.at[s]))
        stores[-1].start()
    for store in stores:
        store.wait()


def payload_call(occ_coef, vir_coef, extra):
    hbm = pl.BlockSpec(memory_space=pltpu.HBM)
    return pl.pallas_call(
        payload_kernel,
        out_shape=jax.ShapeDtypeStruct((NS, PAY, LANES), bf16),
        in_specs=[hbm] * 5,
        out_specs=hbm,
        scratch_shapes=[
            pltpu.VMEM((NS, ROWS, KO), bf16),
            pltpu.VMEM((NS, ROWS, KV), bf16),
            pltpu.VMEM((NS, PAY, LANES), bf16),
        ]
        + [pltpu.VMEM(part.shape, part.dtype) for part in extra]
        + [pltpu.SemaphoreType.DMA((NS + 1, 3)), pltpu.SemaphoreType.DMA((NS,))],
        compiler_params=pltpu.CompilerParams(vmem_limit_bytes=60 << 20),
        cost_estimate=pl.CostEstimate(flops=0, bytes_accessed=6 << 20, transcendentals=0),
        name="coef_payload",
    )(occ_coef, vir_coef, *extra)


def tile_of(parts, kt):
    return parts[0][kt * BB : (kt + 1) * BB] if kt < TO else parts[1][(kt - TO) * BB : (kt - TO + 1) * BB]


def dens_kernel(jobs, tab, pos, mine, other, wts, *refs):
    outs, (own, far, prod) = refs[: len(jobs)], refs[len(jobs) :]
    zl, x, c = pos[0], pos[1], pos[2]
    lane = lax.broadcasted_iota(jnp.int32, (BB, NJ * BB), 1) // BB
    dims = (((1,), (1,)), ((), ()))
    for (k, start, count), out in zip(jobs, outs):

        def per_dest(m, carry, k=k, start=start, out=out):
            d = ((zl + start + m) % NZ) * NX + (x + k) % NX
            base = d * 8
            for j in range(NJ):
                a = pl.multiple_of(tab[base + j, 16] * BLK, BB)
                b = pl.multiple_of(tab[base + j, 17] * BLK + TO * BB, BB)
                parts = (mine[d, pl.ds(a, TO * BB), :], mine[d, pl.ds(b, TV * BB), :])
                for kt in range(KT):
                    block = tile_of(parts, kt).astype(f32) * wts[kt : kt + 1, :]
                    own[j * BB : (j + 1) * BB, kt * LANES : (kt + 1) * LANES] = block.astype(bf16)
            for p in range(NS):
                for q, src in enumerate((mine, other)):
                    e = 2 * p + (c ^ q)
                    a = pl.multiple_of(tab[base, 32 + e] * BLK, BB)
                    b = pl.multiple_of(tab[base, 64 + e] * BLK + TO * BB, BB)
                    to = pl.ds(pl.multiple_of(e * BB, BB), BB)
                    parts = (src[p, pl.ds(a, TO * BB), :], src[p, pl.ds(b, TV * BB), :])
                    for kt in range(KT):
                        far[to, kt * LANES : (kt + 1) * LANES] = tile_of(parts, kt)
            for kind, cols in enumerate((slice(0, KO), slice(KO, KO + KV))):
                prod[kind] = lax.dot_general(
                    far[:, cols], own[:, cols], dims, preferred_element_type=f32
                ).astype(bf16)
            for t in range(NNB):
                picked = [None, None]
                for j in range(NJ):
                    at = pl.multiple_of(tab[base + j, t] * BB, BB)
                    for kind in range(2):
                        row = prod[kind, pl.ds(at, BB), :]
                        picked[kind] = row if j == 0 else jnp.where(lane == j, row, picked[kind])
                for kind in range(2):
                    out[m, kind * TR + t * BB : kind * TR + (t + 1) * BB, :] = picked[kind]
            return carry

        lax.fori_loop(0, count, per_dest, 0)


def dens_call(jobs, tables, pos, mine, other, wts):
    vmem = pl.BlockSpec(memory_space=pltpu.VMEM)
    smem = pl.BlockSpec(memory_space=pltpu.SMEM)
    parts = tuple(jax.ShapeDtypeStruct((job[2], 2 * TR, NJ * BB), bf16) for job in jobs)
    return pl.pallas_call(
        functools.partial(dens_kernel, jobs),
        out_shape=parts,
        in_specs=[smem, smem, vmem, vmem, vmem],
        out_specs=(vmem,) * len(jobs),
        scratch_shapes=[
            pltpu.VMEM((NJ * BB, KO + KV), bf16),
            pltpu.VMEM((32 * BB, KO + KV), bf16),
            pltpu.VMEM((2, 32 * BB, NJ * BB), bf16),
        ],
        compiler_params=pltpu.CompilerParams(vmem_limit_bytes=24 << 20),
        cost_estimate=pl.CostEstimate(
            flops=2 * sum(job[2] for job in jobs) * 512 * 128 * (KO + KV), bytes_accessed=6 << 20, transcendentals=0
        ),
        name="density_partials",
    )(tables, pos, mine, other, wts)


def tile_kernel(
    meta, t0, t1, t2, t3, blocks, own, keep, give, recv, dens, occ_exp, vir_exp, kron, acc, chi, sem
):
    load = pltpu.make_async_copy(blocks, recv, sem)
    load.start()
    total = t0[...].astype(f32) + t1[...].astype(f32) + t2[...].astype(f32) + t3[...].astype(f32)
    dens[...] = total.astype(bf16)
    chi[...] = jnp.zeros_like(chi)
    row = lax.broadcasted_iota(jnp.int32, (NJ * BB, BB * BB), 0)
    col = lax.broadcasted_iota(jnp.int32, (NJ * BB, BB * BB), 1)

    load.wait()

    def per_pair(j, carry):
        hot_occ = (row == j * BB + col // BB).astype(f32).astype(bf16)
        hot_vir = (row == j * BB + col % BB).astype(f32).astype(bf16)
        occ_exp[...] = jnp.dot(dens[0:TR, :], hot_occ, preferred_element_type=f32)
        vir_exp[...] = jnp.dot(dens[TR : 2 * TR, :], hot_vir, preferred_element_type=f32)
        acc[...] = jnp.zeros_like(acc)
        for t in range(NNB):
            buf = t % 2
            vir = vir_exp[t * BB : (t + 1) * BB, :]
            for lam in range(BB):
                occ = jnp.broadcast_to(occ_exp[t * BB + lam : t * BB + lam + 1, :], (BB, BB * BB))
                kron[buf, lam * BB : (lam + 1) * BB, :] = (occ * vir).astype(bf16)
            slot = meta[j * NNB + t]
            aux = meta[128 + j * NNB + t]
            paired = jnp.dot(recv[slot], kron[buf], preferred_element_type=f32)
            acc[aux] = acc[aux] + paired
        target = meta[240 + j]
        rows = acc[...].reshape(NAB * AB, BB * BB).astype(bf16)
        chi[target] += lax.dot_general(
            own[j], rows, (((1,), (1,)), ((), ())), preferred_element_type=f32
        )
        return carry

    lax.fori_loop(0, NJ, per_pair, 0)
    low = lax.broadcasted_iota(jnp.int32, (1, 8, 128), 2) < 64
    first = jnp.full((1, 8, 128), meta[248], jnp.int32) == 0
    for tile in range(4):
        grid = chi[:, :, tile * 128 : (tile + 1) * 128].reshape(NS, 2, 2, 8, 128)
        for side, col in enumerate((2 * tile, 2 * tile + 1)):
            packed = []
            for core in range(2):
                top, bot = grid[:, core, 0], grid[:, core, 1]
                if side == 0:
                    packed.append(jnp.where(low, top, pltpu.roll(bot, 64, 2)))
                else:
                    packed.append(jnp.where(low, pltpu.roll(top, 64, 2), bot))
            keep[:, col] = jnp.where(first, packed[0], packed[1])
            give[:, col] = jnp.where(first, packed[1], packed[0])


def shift(rows, axis, size, k):
    return lax.ppermute(rows, axis, [(i, (i + k) % size) for i in range(size)]) if k else rows


def body(
    occ_coef,
    vir_coef,
    occ_weight,
    vir_weight,
    three_center,
    pair_blocks,
    send_pairs,
    partners,
    partner_blocks,
):
    zl, x, c = lax.axis_index("zl"), lax.axis_index("x"), lax.axis_index("c")
    share = zl * NX + x
    vmem = pl.BlockSpec(memory_space=pltpu.VMEM)
    smem = pl.BlockSpec(memory_space=pltpu.SMEM)
    whole = pl.BlockSpec(memory_space=pl.ANY)
    spread_out = functools.partial(lax.all_to_all, split_axis=0, concat_axis=0, tiled=True)
    extra = (pair_blocks.T, partners, partner_blocks.transpose(2, 0, 1))
    mine = spread_out(payload_call(occ_coef, vir_coef, extra), ("zl", "x"))
    out_blocks = three_center[send_pairs.reshape(-1)]
    wts = jnp.concatenate(
        [
            lax.dynamic_slice_in_dim(occ_weight, share * KO, KO),
            lax.dynamic_slice_in_dim(vir_weight, share * KV, KV),
        ]
    ).reshape(KT, LANES)
    pos = jnp.stack([zl, x, c, share]).astype(jnp.int32)
    mine, out_blocks, wts, pos = lax.optimization_barrier((mine, out_blocks, wts, pos))
    received = spread_out(out_blocks, ("zl", "x", "c"))
    swap = [(0, 1), (1, 0)]
    tables = mine[:, LOCAL * BLK :, :].astype(jnp.int32).reshape(NS * 8, LANES)
    other = lax.ppermute(mine, "c", swap)
    ahead, behind = dens_call(((2, 0, 2), (2, 2, 2)), tables, pos, mine, other, wts)
    ahead, behind = shift(ahead, "x", NX, 1), shift(behind, "x", NX, NX - 1)
    part1, part3, part0 = dens_call(
        ((1, 0, NZ), (3, 0, NZ), (0, 0, NZ)), tables, pos, mine, other, wts
    )
    part1 = jnp.concatenate([(part1[:2].astype(f32) + ahead.astype(f32)).astype(bf16), part1[2:]])
    part3 = jnp.concatenate([part3[:2], (part3[2:].astype(f32) + behind.astype(f32)).astype(bf16)])
    summed = part0.astype(f32)
    summed = summed + shift(part1, "x", NX, 1).astype(f32)
    summed = summed + shift(part3, "x", NX, NX - 1).astype(f32)
    tiles = [shift(summed[m].astype(bf16), "zl", NZ, m) for m in range(NZ)]

    slots = partners.reshape(-1)
    pad = jnp.zeros((32,), jnp.int32)
    far_aux = partner_blocks[:, :, 2].reshape(-1)
    meta = jnp.concatenate(
        [slots, pad, far_aux, pad[:16], pair_blocks[:, 2], c.astype(jnp.int32)[None], pad[:7]]
    )
    half = jax.ShapeDtypeStruct((NS, 8, 8, 128), f32)
    keep, give = pl.pallas_call(
        tile_kernel,
        out_shape=(half, half),
        in_specs=[smem] + [vmem] * 4 + [whole, vmem],
        out_specs=(vmem, vmem),
        scratch_shapes=[
            pltpu.VMEM((32, AB, BB * BB), bf16),
            pltpu.VMEM((2 * TR, NJ * BB), bf16),
            pltpu.VMEM((TR, BB * BB), f32),
            pltpu.VMEM((TR, BB * BB), f32),
            pltpu.VMEM((2, BB * BB, BB * BB), bf16),
            pltpu.VMEM((NAB, AB, BB * BB), f32),
            pltpu.VMEM((NAB, AB, NAB * AB), f32),
            pltpu.SemaphoreType.DMA,
        ],
        compiler_params=pltpu.CompilerParams(vmem_limit_bytes=32 << 20),
        cost_estimate=pl.CostEstimate(
            flops=2 * 96 * 128 * 256 * 256, bytes_accessed=4 << 20, transcendentals=0
        ),
        name="chi_tiles",
    )(meta, *tiles, received, three_center)

    pair_sum = keep + lax.ppermute(give, "c", swap)
    gathered = lax.all_to_all(
        pair_sum.astype(bf16).reshape(128, 8, 128),
        ("zl", "x", "y", "zh"),
        split_axis=0,
        concat_axis=0,
        tiled=True,
    )
    total = jnp.sum(gathered.astype(f32), axis=0)
    return jnp.concatenate([total[:, :64], total[:, 64:]], axis=0)


def solution(mesh):
    fine = Mesh(mesh.devices.reshape(4, 4, 2, 4, 2), ALL)
    return jax.shard_map(
        body,
        mesh=fine,
        in_specs=(
            P(ALL, None),
            P(ALL, None),
            P(),
            P(),
            P(ALL, None, None),
            P(ALL, None),
            P(ALL, None),
            P(ALL, None),
            P(ALL, None, None),
        ),
        out_specs=P(("zl", "x", "c"), ("y", "zh")),
        check_vma=False,
    )
```

time: 187 us -> 176 us (0.941); the launches traced: 184 us -> 175 us
  starting transfers between devices: 39.1 us -> 28.6 us
  Pallas kernels: 22.8 us -> 30.1 us
  blocking collectives: 32.3 us -> 26.8 us
  waiting for transfers between devices: 79.4 us -> 83.1 us
    all_to_all x2, waiting for transfers between devices: 0.01 us -> 57.6 us  [the longest x1 57.6 us: body(): mine = spread_out(payload_call(occ_coef, vir_coef, extra), ('zl', 'x'))]
    ppermute x13 -> x9, waiting for transfers between devices: 79.4 us -> 25.5 us  [the longest x7 23.6 us: shift(): lax.ppermute(rows, axis, [(i, (i + k) % size) for i in range(size)])]
    ppermute x13 -> x9, starting transfers between devices: 23.7 us -> 12.8 us  [the longest x7 12.7 us: shift(): lax.ppermute(rows, axis, [(i, (i + k) % size) for i in range(size)])]
    pallas_call x2 -> x4, Pallas kernels: 22.8 us -> 30.1 us  [the longest x2 17.5 us: dens_call(): pl.pallas_call(functools.partial(dens_kernel, jobs), out_shape=parts, in_...]
    all_to_all x1, blocking collectives: 32.3 us -> 26.8 us  [body(): lax.all_to_all(pair_sum.astype(bf16).reshape(128, 8, 128), ('zl', 'x', 'y...]
    reshape x4 -> x0, local copies, waits for them, and re-layouts: 3.01 us -> none  [the longest x1 1.72 us: body(): vir_coef.reshape(ROWS, NS, KV).transpose(1, 0, 2)]
  transfers between devices with their start and end apart: 15 -> 11, of which waited for: 10 -> 8; matrix products, arithmetic and copies ran while one was open for 2% -> 3% of each run, Pallas kernels for 8% -> 10%
where the time goes in v2:
time: 176 us; the launch traced here: 175 us
  waiting for transfers between devices  83.1 us (47%)
  Pallas kernels  30.1 us (17%)
  starting transfers between devices  28.6 us (16%)
  blocking collectives  26.8 us (15%)
  local copies, waits for them, and re-layouts  5.35 us (3%)
    all_to_all x1, waiting for transfers between devices, body(): mine = spread_out(payload_call(occ_coef, vir_coef, extra), ('zl', 'x'))  57.6 us
    all_to_all x1, blocking collectives, body(): lax.all_to_all(pair_sum.astype(bf16).reshape(128, 8, 128), ('zl', 'x', 'y...  26.8 us
    ppermute x7, waiting for transfers between devices, shift(): lax.ppermute(rows, axis, [(i, (i + k) % size) for i in range(size)])  23.6 us
    pallas_call x2, Pallas kernels, dens_call(): pl.pallas_call(functools.partial(dens_kernel, jobs), out_shape=parts, in_...  17.5 us
    ppermute x7, starting transfers between devices, shift(): lax.ppermute(rows, axis, [(i, (i + k) % size) for i in range(size)])  12.7 us
    pallas_call x1, Pallas kernels, body(): pl.pallas_call(tile_kernel, out_shape=(half, half), in_specs=[smem] + [vm...  9.39 us
    all_to_all x1, starting transfers between devices, body(): mine = spread_out(payload_call(occ_coef, vir_coef, extra), ('zl', 'x'))  8.63 us
    all_to_all x1, starting transfers between devices, body(): received = spread_out(out_blocks, ('zl', 'x', 'c'))  7.2 us
  transfers between devices with their start and end apart: 11, of which 8 were waited for; matrix products, arithmetic and copies ran while one was open for 3% of the time, Pallas kernels for 10%

profile of v2, /device:TPU:32, one launch (start us, length us, event | category | flops | bytes accessed | tf_op | source)
XLA Modules:
  0.0 175.5 jit_solution(11532131276709172903)
XLA Ops:
  0.0 3.3 %coef_payload.1 = bf16[16,680,128]{2,1,0:T(8,128)(2,1)} custom-call(bf16[96,4096]{1,0:T(8,128)(2,1)} %occ.1, bf16[96,10240]{1,0:T(8,128)(2,1)} %vir.1, s32[3,8]{1,0:T(4,128)} %bitcast.28, s32[8,12]{1,0:T(8,128)} %refs_1_.1, s32[3,8,12]{2,1,0:T(8,128)} %bitcast.27), custom_call_target="tpu_custom_call" | custom-call | bytes 6291456 | tf_op jit(solution)/shard_map/coef_payload/pallas_call | solution.py:94
  3.3 0.0 copy-start.2
  3.3 0.0 copy-start
  3.3 8.6 %all-to-all-start = ((bf16[16,680,128]{2,1,0:T(8,128)(2,1)}), bf16[16,680,128]{2,1,0:T(8,128)(2,1)S(1)}, u32[]{:S(2)}, u32[]{:S(2)}) async-start(bf16[16,680,128]{2,1,0:T(8,128)(2,1)} %coef_payload.1), calls=%async_computation | async-start | bytes 5570560 | tf_op jit(solution)/shard_map/all_to_all | solution.py:257
  11.9 0.8 dynamic_slice.7
  12.7 0.8 dynamic_slice.6
  13.4 0.0 copy-done.2
  13.5 0.0 copy-done
  13.5 2.1 %gather_fusion = bf16[32,128,256]{2,1,0:T(8,128)(2,1)} fusion(bf16[8,128,256]{2,1,0:T(8,128)(2,1)S(1)} %copy-done, s32[1024]{0:T(1024)S(1)} %pad_clamp_fusion), kind=kCustom, calls=%fused_computation | custom fusion | bytes 4194432 | tf_op jit(solution)/shard_map/gather | solution.py:258
  15.5 0.1 pad_add_fusion.pos
  15.6 57.6 %all-to-all-done.mine = bf16[16,680,128]{2,1,0:T(8,128)(2,1)S(1)} async-done(((bf16[16,680,128]{2,1,0:T(8,128)(2,1)}), bf16[16,680,128]{2,1,0:T(8,128)(2,1)S(1)}, u32[]{:S(2)}, u32[]{:S(2)}) %all-to-all-start) | async-done | bytes 2785312 | tf_op jit(solution)/shard_map/all_to_all | solution.py:257
  73.2 0.0 collective-permute-start
  73.2 7.2 %all-to-all-start.1 = ((bf16[32,128,256]{2,1,0:T(8,128)(2,1)}), bf16[32,128,256]{2,1,0:T(8,128)(2,1)}, u32[]{:S(2)}, u32[]{:S(2)}) async-start(bf16[32,128,256]{2,1,0:T(8,128)(2,1)} %gather_fusion), calls=%async_computation.1 | async-start | bytes 4194304 | tf_op jit(solution)/shard_map/all_to_all | solution.py:267
  80.4 0.0 collective-permute-done.other
  80.4 5.3 %density_partials.3 = (bf16[2,384,128]{2,1,0:T(8,128)(2,1)S(1)}, bf16[2,384,128]{2,1,0:T(8,128)(2,1)S(1)}) custom-call(s32[128,128]{1,0:T(8,128)S(1)} %bitcast_convert_fusion.tab, s32[4]{0:T(128)S(1)} %pad_add_fusion.pos, bf16[16,680,128]{2,1,0:T(8,128)(2,1)S(1)} %all-to-all-done.mine, bf16[16,680,128]{2,1,0:T(8,128)(2,1)} %collective-permute-done.other, ...), custom_call_target="tpu_custom_call" | custom-call | flops 469762048 | bytes 6291456 | tf_op jit(solution)/shard_map/density_partials/pallas_call | solution.py:164
  85.8 1.6 collective-permute-start.1
  87.3 12.2 %density_partials.2 = (bf16[4,384,128]{2,1,0:T(8,128)(2,1)S(1)}, bf16[4,384,128]{2,1,0:T(8,128)(2,1)S(1)}, bf16[4,384,128]{2,1,0:T(8,128)(2,1)S(1)}) custom-call(s32[128,128]{1,0:T(8,128)S(1)} %bitcast_convert_fusion.tab, s32[4]{0:T(128)S(1)} %pad_add_fusion.pos, bf16[16,680,128]{2,1,0:T(8,128)(2,1)S(1)} %all-to-all-done.mine, ...), custom_call_target="tpu_custom_call" | custom-call | flops 1409286144 | bytes 6291456 | tf_op jit(solution)/shard_map/density_partials/pallas_call | solution.py:164
  99.5 1.8 %collective-permute-start.3 = (bf16[2,384,128]{2,1,0:T(8,128)(2,1)S(1)}, bf16[2,384,128]{2,1,0:T(8,128)(2,1)S(1)}, u32[]{:S(2)}, u32[]{:S(2)}) collective-permute-start(bf16[2,384,128]{2,1,0:T(8,128)(2,1)S(1)} %get-tuple-element.23), channel_id=1, source_target_pairs={{0,48},{16,0},{32,16},{48,32},{1,49},{17,1},{33,17},{49,33},{2,50}... | collective-permute-start | bytes 589832 | tf_op jit(solution)/shard_map/ppermute | solution.py:236
  101.3 0.0 collective-permute-done.1
  101.3 0.1 add_convert_fusion.3
  101.4 0.0 copy-start.1
  101.5 0.3 collective-permute-start.2
  101.8 7.5 %collective-permute-done.3 = bf16[2,384,128]{2,1,0:T(8,128)(2,1)S(1)} collective-permute-done((bf16[2,384,128]{2,1,0:T(8,128)(2,1)S(1)}, bf16[2,384,128]{2,1,0:T(8,128)(2,1)S(1)}, u32[]{:S(2)}, u32[]{:S(2)}) %collective-permute-start.3) | collective-permute-done | bytes 196640 | tf_op jit(solution)/shard_map/ppermute | solution.py:236
  109.3 0.1 add_convert_fusion.2
  109.4 3.5 %collective-permute-start.4 = (bf16[4,384,128]{2,1,0:T(8,128)(2,1)S(1)}, bf16[4,384,128]{2,1,0:T(8,128)(2,1)S(1)}, u32[]{:S(2)}, u32[]{:S(2)}) collective-permute-start(bf16[4,384,128]{2,1,0:T(8,128)(2,1)S(1)} %pad_maximum_fusion.1), channel_id=1, source_target_pairs={{0,48},{16,0},{32,16},{48,32},{1,49},{17,1},{33,17},{49,33},{2,50}... | collective-permute-start | bytes 1179656 | tf_op jit(solution)/shard_map/ppermute | solution.py:236
  113.0 6.2 %collective-permute-done.2 = bf16[4,384,128]{2,1,0:T(8,128)(2,1)S(1)} collective-permute-done((bf16[4,384,128]{2,1,0:T(8,128)(2,1)S(1)}, bf16[4,384,128]{2,1,0:T(8,128)(2,1)S(1)}, u32[]{:S(2)}, u32[]{:S(2)}) %collective-permute-start.2) | collective-permute-done | bytes 393248 | tf_op jit(solution)/shard_map/ppermute | solution.py:236
  119.2 3.7 %collective-permute-done.4 = bf16[4,384,128]{2,1,0:T(8,128)(2,1)S(1)} collective-permute-done((bf16[4,384,128]{2,1,0:T(8,128)(2,1)S(1)}, bf16[4,384,128]{2,1,0:T(8,128)(2,1)S(1)}, u32[]{:S(2)}, u32[]{:S(2)}) %collective-permute-start.4) | collective-permute-done | bytes 393248 | tf_op jit(solution)/shard_map/ppermute | solution.py:236
  122.9 0.2 add_convert_fusion
  123.1 3.9 %collective-permute-start.5 = (bf16[384,128]{1,0:T(8,128)(2,1)S(1)}, bf16[384,128]{1,0:T(8,128)(2,1)S(1)}, u32[]{:S(2)}, u32[]{:S(2)}) collective-permute-start(bf16[384,128]{1,0:T(8,128)(2,1)S(1)} %get-tuple-element.29), channel_id=1, source_target_pairs={{0,64},{64,128},{128,192},{192,0},{1,65},{65,129},{129,193},{193,1... | collective-permute-start | bytes 294920 | tf_op jit(solution)/shard_map/ppermute | solution.py:236
  127.0 0.0 collective-permute-start.6
  127.0 1.6 collective-permute-start.7
  128.6 0.7 slice_bitcast_fusion.4
  129.2 0.7 slice.43
  129.9 0.0 copy-done.1
  129.9 0.1 reshape.19
  130.0 0.1 reshape_squeeze.3
  130.1 0.1 concatenate.15.meta
  130.2 3.8 %collective-permute-done.5.t1 = bf16[384,128]{1,0:T(8,128)(2,1)S(1)} collective-permute-done((bf16[384,128]{1,0:T(8,128)(2,1)S(1)}, bf16[384,128]{1,0:T(8,128)(2,1)S(1)}, u32[]{:S(2)}, u32[]{:S(2)}) %collective-permute-start.5) | collective-permute-done | bytes 98336 | tf_op jit(solution)/shard_map/ppermute | solution.py:236
  134.0 1.1 collective-permute-done.6.t2
  135.0 1.3 collective-permute-done.7.t3
  136.3 0.0 all-to-all-done.1.blocks
  136.3 9.4 %chi_tiles.1 = (f32[16,8,8,128]{3,2,1,0:T(8,128)S(1)}, f32[16,8,8,128]{3,2,1,0:T(8,128)S(1)}) custom-call(s32[256]{0:T(256)S(1)} %concatenate.15.meta, bf16[384,128]{1,0:T(8,128)(2,1)S(1)} %get-tuple-element.30.t0, bf16[384,128]{1,0:T(8,128)(2,1)S(1)} %collective-permute-done.5.t1, bf16[384,128]{1,0:T(8,128)(2,1)S(1)} %collective-permute-done.6.t2, ...), custom_call_target="tpu_custom_call" | custom-call | flops 1610612736 | bytes 4194304 | tf_op jit(solution)/shard_map/chi_tiles/pallas_call | solution.py:290
  145.7 0.1 collective-permute-start.8
  145.8 1.9 %collective-permute-done.8 = f32[16,8,8,128]{3,2,1,0:T(8,128)S(1)} collective-permute-done((f32[16,8,8,128]{3,2,1,0:T(8,128)S(1)}, f32[16,8,8,128]{3,2,1,0:T(8,128)S(1)}, u32[]{:S(2)}, u32[]{:S(2)}) %collective-permute-start.8) | collective-permute-done | bytes 524320 | tf_op jit(solution)/shard_map/ppermute | solution.py:312
  147.7 0.1 add_convert_fusion.1
  147.8 26.8 %all_to_all.15 = bf16[128,8,128]{2,1,0:T(8,128)(2,1)S(1)} all-to-all(bf16[128,8,128]{2,1,0:T(8,128)(2,1)S(1)} %bitcast.26), channel_id=1, replica_groups=mesh['zl'=4,'x'=4,'c'=2,'y'=4,'zh'=2] {'zl','x','y','zh'}, dimensions={0} | all-to-all | bytes 524288 | tf_op jit(solution)/shard_map/all_to_all | solution.py:313
  174.6 0.1 convert_reduce_fusion
  174.8 0.1 fusion.1
  174.8 0.6 pad_maximum_fusion.2
  (12 shorter events, 0.2 us)
Async XLA Ops:
  3.3 10.2 %copy-start.2 = (s32[32,1]{0,1:T(1,128)S(1)}, s32[32,1]{0,1:T(1,128)}, u32[]{:S(2)}) copy-start(s32[32,1]{0,1:T(1,128)} %param.15) | copy-start | bytes 388
  3.3 10.2 %copy-start = (bf16[8,128,256]{2,1,0:T(8,128)(2,1)S(1)}, bf16[8,128,256]{2,1,0:T(8,128)(2,1)}, u32[]{:S(2)}) copy-start(bf16[8,128,256]{2,1,0:T(8,128)(2,1)} %own.1) | copy-start | bytes 1572868
  3.3 69.9 %all-to-all-start = ((bf16[16,680,128]{2,1,0:T(8,128)(2,1)}), bf16[16,680,128]{2,1,0:T(8,128)(2,1)S(1)}, u32[]{:S(2)}, u32[]{:S(2)}) async-start(bf16[16,680,128]{2,1,0:T(8,128)(2,1)} %coef_payload.1), calls=%async_computation | async-start | bytes 5570560 | tf_op jit(solution)/shard_map/all_to_all | solution.py:257
  73.2 7.2 %collective-permute-start = (bf16[16,680,128]{2,1,0:T(8,128)(2,1)S(1)}, bf16[16,680,128]{2,1,0:T(8,128)(2,1)}, u32[]{:S(2)}, u32[]{:S(2)}) collective-permute-start(bf16[16,680,128]{2,1,0:T(8,128)(2,1)S(1)} %all-to-all-done.mine), channel_id=1, source_target_pairs={{0,8},{8,0},{1,9},{9,1},{2,10},{10,2},{3,11},{11,3},{4,12},{12,4},... | collective-permute-start | bytes 8355848 | tf_op jit(solution)/shard_map/ppermute | solution.py:270
  73.2 63.1 %all-to-all-start.1 = ((bf16[32,128,256]{2,1,0:T(8,128)(2,1)}), bf16[32,128,256]{2,1,0:T(8,128)(2,1)}, u32[]{:S(2)}, u32[]{:S(2)}) async-start(bf16[32,128,256]{2,1,0:T(8,128)(2,1)} %gather_fusion), calls=%async_computation.1 | async-start | bytes 4194304 | tf_op jit(solution)/shard_map/all_to_all | solution.py:267
  85.8 15.6 %collective-permute-start.1 = (bf16[2,384,128]{2,1,0:T(8,128)(2,1)S(1)}, bf16[2,384,128]{2,1,0:T(8,128)(2,1)S(1)}, u32[]{:S(2)}, u32[]{:S(2)}) collective-permute-start(bf16[2,384,128]{2,1,0:T(8,128)(2,1)S(1)} %get-tuple-element.21), channel_id=1, source_target_pairs={{0,16},{16,32},{32,48},{48,0},{1,17},{17,33},{33,49},{49,1},{2,18}... | collective-permute-start | bytes 589832 | tf_op jit(solution)/shard_map/ppermute | solution.py:236
  99.5 9.8 %collective-permute-start.3 = (bf16[2,384,128]{2,1,0:T(8,128)(2,1)S(1)}, bf16[2,384,128]{2,1,0:T(8,128)(2,1)S(1)}, u32[]{:S(2)}, u32[]{:S(2)}) collective-permute-start(bf16[2,384,128]{2,1,0:T(8,128)(2,1)S(1)} %get-tuple-element.23), channel_id=1, source_target_pairs={{0,48},{16,0},{32,16},{48,32},{1,49},{17,1},{33,17},{49,33},{2,50}... | collective-permute-start | bytes 589832 | tf_op jit(solution)/shard_map/ppermute | solution.py:236
  101.4 28.5 %copy-start.1 = (s32[8,12]{1,0:T(8,128)S(1)}, s32[8,12]{1,0:T(8,128)}, u32[]{:S(2)}) copy-start(s32[8,12]{1,0:T(8,128)} %refs_1_.1) | copy-start | bytes 1156
  101.5 17.7 %collective-permute-start.2 = (bf16[4,384,128]{2,1,0:T(8,128)(2,1)S(1)}, bf16[4,384,128]{2,1,0:T(8,128)(2,1)S(1)}, u32[]{:S(2)}, u32[]{:S(2)}) collective-permute-start(bf16[4,384,128]{2,1,0:T(8,128)(2,1)S(1)} %pad_maximum_fusion), channel_id=1, source_target_pairs={{0,16},{16,32},{32,48},{48,0},{1,17},{17,33},{33,49},{49,1},{2,18}... | collective-permute-start | bytes 1179656 | tf_op jit(solution)/shard_map/ppermute | solution.py:236
  109.4 13.4 %collective-permute-start.4 = (bf16[4,384,128]{2,1,0:T(8,128)(2,1)S(1)}, bf16[4,384,128]{2,1,0:T(8,128)(2,1)S(1)}, u32[]{:S(2)}, u32[]{:S(2)}) collective-permute-start(bf16[4,384,128]{2,1,0:T(8,128)(2,1)S(1)} %pad_maximum_fusion.1), channel_id=1, source_target_pairs={{0,48},{16,0},{32,16},{48,32},{1,49},{17,1},{33,17},{49,33},{2,50}... | collective-permute-start | bytes 1179656 | tf_op jit(solution)/shard_map/ppermute | solution.py:236
  123.1 10.9 %collective-permute-start.5 = (bf16[384,128]{1,0:T(8,128)(2,1)S(1)}, bf16[384,128]{1,0:T(8,128)(2,1)S(1)}, u32[]{:S(2)}, u32[]{:S(2)}) collective-permute-start(bf16[384,128]{1,0:T(8,128)(2,1)S(1)} %get-tuple-element.29), channel_id=1, source_target_pairs={{0,64},{64,128},{128,192},{192,0},{1,65},{65,129},{129,193},{193,1... | collective-permute-start | bytes 294920 | tf_op jit(solution)/shard_map/ppermute | solution.py:236
  127.0 8.0 %collective-permute-start.6 = (bf16[384,128]{1,0:T(8,128)(2,1)S(1)}, bf16[384,128]{1,0:T(8,128)(2,1)S(1)}, u32[]{:S(2)}, u32[]{:S(2)}) collective-permute-start(bf16[384,128]{1,0:T(8,128)(2,1)S(1)} %get-tuple-element.28), channel_id=1, source_target_pairs={{0,128},{64,192},{128,0},{192,64},{1,129},{65,193},{129,1},{193,65... | collective-permute-start | bytes 294920 | tf_op jit(solution)/shard_map/ppermute | solution.py:236
  127.0 9.3 %collective-permute-start.7 = (bf16[384,128]{1,0:T(8,128)(2,1)S(1)}, bf16[384,128]{1,0:T(8,128)(2,1)S(1)}, u32[]{:S(2)}, u32[]{:S(2)}) collective-permute-start(bf16[384,128]{1,0:T(8,128)(2,1)S(1)} %get-tuple-element.27), channel_id=1, source_target_pairs={{0,192},{64,0},{128,64},{192,128},{1,193},{65,1},{129,65},{193,129... | collective-permute-start | bytes 294920 | tf_op jit(solution)/shard_map/ppermute | solution.py:236
  145.7 2.0 %collective-permute-start.8 = (f32[16,8,8,128]{3,2,1,0:T(8,128)S(1)}, f32[16,8,8,128]{3,2,1,0:T(8,128)S(1)}, u32[]{:S(2)}, u32[]{:S(2)}) collective-permute-start(f32[16,8,8,128]{3,2,1,0:T(8,128)S(1)} %get-tuple-element.26), channel_id=1, source_target_pairs={{0,8},{8,0},{1,9},{9,1},{2,10},{10,2},{3,11},{11,3},{4,12},{12,4},... | collective-permute-start | bytes 1572872 | tf_op jit(solution)/shard_map/ppermute | solution.py:312

commit v3 on v2

--- a/solution.py
+++ b/solution.py
@@ -26,7 +26,9 @@
 KT = TO + TV
 BLK = KT * BB
 PAY = LOCAL * BLK + 8
-ALL = ("zl", "x", "c", "y", "zh")
+ZL = ("zb", "za")
+ZX = ("zb", "za", "x")
+ALL = ("zb", "za", "x", "c", "y", "zh")
 f32 = jnp.float32
 bf16 = jnp.bfloat16
 
@@ -114,78 +116,95 @@
 
 
 def dens_kernel(jobs, tab, pos, mine, other, wts, *refs):
-    outs, (own, far, prod) = refs[: len(jobs)], refs[len(jobs) :]
+    outs, scratch = refs[: len(jobs)], refs[len(jobs) :]
     zl, x, c = pos[0], pos[1], pos[2]
     lane = lax.broadcasted_iota(jnp.int32, (BB, NJ * BB), 1) // BB
     dims = (((1,), (1,)), ((), ()))
-    for (k, start, count), out in zip(jobs, outs):
-
-        def per_dest(m, carry, k=k, start=start, out=out):
-            d = ((zl + start + m) % NZ) * NX + (x + k) % NX
-            base = d * 8
+
+    def gather(d, own, far):
+        base = d * 8
+        for j in range(NJ):
+            a = pl.multiple_of(tab[base + j, 16] * BLK, BB)
+            b = pl.multiple_of(tab[base + j, 17] * BLK + TO * BB, BB)
+            parts = (mine[d, pl.ds(a, TO * BB), :], mine[d, pl.ds(b, TV * BB), :])
+            for kt in range(KT):
+                block = tile_of(parts, kt).astype(f32) * wts[kt : kt + 1, :]
+                own[j * BB : (j + 1) * BB, kt * LANES : (kt + 1) * LANES] = block.astype(bf16)
+        for p in range(NS):
+            for q, src in enumerate((mine, other)):
+                e = 2 * p + (c ^ q)
+                a = pl.multiple_of(tab[base, 32 + e] * BLK, BB)
+                b = pl.multiple_of(tab[base, 64 + e] * BLK + TO * BB, BB)
+                to = pl.ds(pl.multiple_of(e * BB, BB), BB)
+                parts = (src[p, pl.ds(a, TO * BB), :], src[p, pl.ds(b, TV * BB), :])
+                for kt in range(KT):
+                    far[to, kt * LANES : (kt + 1) * LANES] = tile_of(parts, kt)
+
+    def multiply(own, far, prod):
+        for kind, cols in enumerate((slice(0, KO), slice(KO, KO + KV))):
+            prod[kind] = lax.dot_general(
+                far[:, cols], own[:, cols], dims, preferred_element_type=f32
+            ).astype(bf16)
+
+    def select(d, m, prod, out):
+        base = d * 8
+        for t in range(NNB):
+            picked = [None, None]
             for j in range(NJ):
-                a = pl.multiple_of(tab[base + j, 16] * BLK, BB)
-                b = pl.multiple_of(tab[base + j, 17] * BLK + TO * BB, BB)
-                parts = (mine[d, pl.ds(a, TO * BB), :], mine[d, pl.ds(b, TV * BB), :])
-                for kt in range(KT):
-                    block = tile_of(parts, kt).astype(f32) * wts[kt : kt + 1, :]
-                    own[j * BB : (j + 1) * BB, kt * LANES : (kt + 1) * LANES] = block.astype(bf16)
-            for p in range(NS):
-                for q, src in enumerate((mine, other)):
-                    e = 2 * p + (c ^ q)
-                    a = pl.multiple_of(tab[base, 32 + e] * BLK, BB)
-                    b = pl.multiple_of(tab[base, 64 + e] * BLK + TO * BB, BB)
-                    to = pl.ds(pl.multiple_of(e * BB, BB), BB)
-                    parts = (src[p, pl.ds(a, TO * BB), :], src[p, pl.ds(b, TV * BB), :])
-                    for kt in range(KT):
-                        far[to, kt * LANES : (kt + 1) * LANES] = tile_of(parts, kt)
-            for kind, cols in enumerate((slice(0, KO), slice(KO, KO + KV))):
-                prod[kind] = lax.dot_general(
-                    far[:, cols], own[:, cols], dims, preferred_element_type=f32
-                ).astype(bf16)
-            for t in range(NNB):
-                picked = [None, None]
-                for j in range(NJ):
-                    at = pl.multiple_of(tab[base + j, t] * BB, BB)
-                    for kind in range(2):
-                        row = prod[kind, pl.ds(at, BB), :]
-                        picked[kind] = row if j == 0 else jnp.where(lane == j, row, picked[kind])
+                at = pl.multiple_of(tab[base + j, t] * BB, BB)
                 for kind in range(2):
-                    out[m, kind * TR + t * BB : kind * TR + (t + 1) * BB, :] = picked[kind]
+                    row = prod[kind, pl.ds(at, BB), :]
+                    picked[kind] = row if j == 0 else jnp.where(lane == j, row, picked[kind])
+            for kind in range(2):
+                out[m, kind * TR + t * BB : kind * TR + (t + 1) * BB, :] = picked[kind]
+
+    for k, out in zip(jobs, outs):
+
+        def per_two(i, carry, k=k, out=out):
+            ms = (2 * i, 2 * i + 1)
+            ds = [(zl ^ (2 * n + i)) * NX + (x + k) % NX for n in range(2)]
+            for n in range(2):
+                gather(ds[n], scratch[n], scratch[2 + n])
+            for n in range(2):
+                multiply(scratch[n], scratch[2 + n], scratch[4 + n])
+            for n in range(2):
+                select(ds[n], ms[n], scratch[4 + n], out)
             return carry
 
-        lax.fori_loop(0, count, per_dest, 0)
+        lax.fori_loop(0, NZ // 2, per_two, 0)
 
 
 def dens_call(jobs, tables, pos, mine, other, wts):
     vmem = pl.BlockSpec(memory_space=pltpu.VMEM)
     smem = pl.BlockSpec(memory_space=pltpu.SMEM)
-    parts = tuple(jax.ShapeDtypeStruct((job[2], 2 * TR, NJ * BB), bf16) for job in jobs)
+    part = jax.ShapeDtypeStruct((NZ, 2 * TR, NJ * BB), bf16)
     return pl.pallas_call(
         functools.partial(dens_kernel, jobs),
-        out_shape=parts,
+        out_shape=(part,) * len(jobs),
         in_specs=[smem, smem, vmem, vmem, vmem],
         out_specs=(vmem,) * len(jobs),
         scratch_shapes=[
             pltpu.VMEM((NJ * BB, KO + KV), bf16),
+            pltpu.VMEM((NJ * BB, KO + KV), bf16),
             pltpu.VMEM((32 * BB, KO + KV), bf16),
+            pltpu.VMEM((32 * BB, KO + KV), bf16),
+            pltpu.VMEM((2, 32 * BB, NJ * BB), bf16),
             pltpu.VMEM((2, 32 * BB, NJ * BB), bf16),
         ],
         compiler_params=pltpu.CompilerParams(vmem_limit_bytes=24 << 20),
         cost_estimate=pl.CostEstimate(
-            flops=2 * sum(job[2] for job in jobs) * 512 * 128 * (KO + KV), bytes_accessed=6 << 20, transcendentals=0
+            flops=2 * len(jobs) * NZ * 512 * 128 * (KO + KV), bytes_accessed=6 << 20, transcendentals=0
         ),
         name="density_partials",
     )(tables, pos, mine, other, wts)
 
 
 def tile_kernel(
-    meta, t0, t1, t2, t3, blocks, own, keep, give, recv, dens, occ_exp, vir_exp, kron, acc, chi, sem
+    meta, kept, moved, blocks, own, keep, give, recv, dens, occ_exp, vir_exp, kron, acc, chi, sem
 ):
     load = pltpu.make_async_copy(blocks, recv, sem)
     load.start()
-    total = t0[...].astype(f32) + t1[...].astype(f32) + t2[...].astype(f32) + t3[...].astype(f32)
-    dens[...] = total.astype(bf16)
+    dens[...] = (kept[...] + moved[...].astype(f32)).astype(bf16)
     chi[...] = jnp.zeros_like(chi)
     row = lax.broadcasted_iota(jnp.int32, (NJ * BB, BB * BB), 0)
     col = lax.broadcasted_iota(jnp.int32, (NJ * BB, BB * BB), 1)
@@ -200,10 +219,10 @@
         acc[...] = jnp.zeros_like(acc)
         for t in range(NNB):
             buf = t % 2
-            vir = vir_exp[t * BB : (t + 1) * BB, :]
+            vir = vir_exp[t * BB : (t + 1) * BB, :].astype(bf16)
             for lam in range(BB):
                 occ = jnp.broadcast_to(occ_exp[t * BB + lam : t * BB + lam + 1, :], (BB, BB * BB))
-                kron[buf, lam * BB : (lam + 1) * BB, :] = (occ * vir).astype(bf16)
+                kron[buf, lam * BB : (lam + 1) * BB, :] = occ.astype(bf16) * vir
             slot = meta[j * NNB + t]
             aux = meta[128 + j * NNB + t]
             paired = jnp.dot(recv[slot], kron[buf], preferred_element_type=f32)
@@ -247,15 +266,25 @@
     partners,
     partner_blocks,
 ):
-    zl, x, c = lax.axis_index("zl"), lax.axis_index("x"), lax.axis_index("c")
+    zl, x, c = lax.axis_index(ZL), lax.axis_index("x"), lax.axis_index("c")
     share = zl * NX + x
     vmem = pl.BlockSpec(memory_space=pltpu.VMEM)
     smem = pl.BlockSpec(memory_space=pltpu.SMEM)
     whole = pl.BlockSpec(memory_space=pl.ANY)
     spread_out = functools.partial(lax.all_to_all, split_axis=0, concat_axis=0, tiled=True)
     extra = (pair_blocks.T, partners, partner_blocks.transpose(2, 0, 1))
-    mine = spread_out(payload_call(occ_coef, vir_coef, extra), ("zl", "x"))
-    out_blocks = three_center[send_pairs.reshape(-1)]
+    mine = spread_out(payload_call(occ_coef, vir_coef, extra), ZX)
+    flip = [(0, 1), (1, 0)]
+    step = jnp.arange(NX, dtype=jnp.int32)
+    to_row = step[None, :] * (2 * NX) + ((x + step)[:, None] % NX) * 2
+    sends = send_pairs.reshape(-1)
+    kept = three_center[sends[(to_row + c).reshape(-1)]]
+    given = three_center[sends[(to_row + 1 - c).reshape(-1)]]
+    given = lax.ppermute(given, "c", flip)
+    blocks = (NX, NZ, AB, BB * BB)
+    kept, given = kept.reshape(blocks), given.reshape(blocks)
+    by_x = [shift(jnp.stack([kept[k], given[k]]), "x", NX, k) for k in range(NX)]
+    by_z = jnp.stack(by_x).transpose(2, 0, 1, 3, 4).reshape(32, AB, BB * BB)
     wts = jnp.concatenate(
         [
             lax.dynamic_slice_in_dim(occ_weight, share * KO, KO),
@@ -263,34 +292,34 @@
         ]
     ).reshape(KT, LANES)
     pos = jnp.stack([zl, x, c, share]).astype(jnp.int32)
-    mine, out_blocks, wts, pos = lax.optimization_barrier((mine, out_blocks, wts, pos))
-    received = spread_out(out_blocks, ("zl", "x", "c"))
-    swap = [(0, 1), (1, 0)]
+    mine, by_z, wts, pos = lax.optimization_barrier((mine, by_z, wts, pos))
+    received = spread_out(by_z, ZL)
     tables = mine[:, LOCAL * BLK :, :].astype(jnp.int32).reshape(NS * 8, LANES)
-    other = lax.ppermute(mine, "c", swap)
-    ahead, behind = dens_call(((2, 0, 2), (2, 2, 2)), tables, pos, mine, other, wts)
-    ahead, behind = shift(ahead, "x", NX, 1), shift(behind, "x", NX, NX - 1)
-    part1, part3, part0 = dens_call(
-        ((1, 0, NZ), (3, 0, NZ), (0, 0, NZ)), tables, pos, mine, other, wts
-    )
-    part1 = jnp.concatenate([(part1[:2].astype(f32) + ahead.astype(f32)).astype(bf16), part1[2:]])
-    part3 = jnp.concatenate([part3[:2], (part3[2:].astype(f32) + behind.astype(f32)).astype(bf16)])
+    other = lax.ppermute(mine, "c", flip)
+    (part2,) = dens_call((2,), tables, pos, mine, other, wts)
+    part2 = shift(part2, "x", NX, 1)
+    part1, part3, part0 = dens_call((1, 3, 0), tables, pos, mine, other, wts)
+    part1 = (part1.astype(f32) + part2.astype(f32)).astype(bf16)
     summed = part0.astype(f32)
     summed = summed + shift(part1, "x", NX, 1).astype(f32)
     summed = summed + shift(part3, "x", NX, NX - 1).astype(f32)
-    tiles = [shift(summed[m].astype(bf16), "zl", NZ, m) for m in range(NZ)]
+    crossed = lax.ppermute(summed[2:].astype(bf16), "za", flip).astype(f32)
+    kept_tiles = summed[0] + crossed[0]
+    moved_tiles = lax.ppermute((summed[1] + crossed[1]).astype(bf16), "zb", flip)
 
     slots = partners.reshape(-1)
+    lag_x = (x - slots // 2 % NX) % NX
+    place = (slots // (2 * NX) * NX + lag_x) * 2 + ((slots % 2) ^ c)
     pad = jnp.zeros((32,), jnp.int32)
     far_aux = partner_blocks[:, :, 2].reshape(-1)
     meta = jnp.concatenate(
-        [slots, pad, far_aux, pad[:16], pair_blocks[:, 2], c.astype(jnp.int32)[None], pad[:7]]
+        [place, pad, far_aux, pad[:16], pair_blocks[:, 2], c.astype(jnp.int32)[None], pad[:7]]
     )
-    half = jax.ShapeDtypeStruct((NS, 8, 8, 128), f32)
+    out_half = jax.ShapeDtypeStruct((NS, 8, 8, 128), f32)
     keep, give = pl.pallas_call(
         tile_kernel,
-        out_shape=(half, half),
-        in_specs=[smem] + [vmem] * 4 + [whole, vmem],
+        out_shape=(out_half, out_half),
+        in_specs=[smem, vmem, vmem, whole, vmem],
         out_specs=(vmem, vmem),
         scratch_shapes=[
             pltpu.VMEM((32, AB, BB * BB), bf16),
@@ -307,12 +336,12 @@
             flops=2 * 96 * 128 * 256 * 256, bytes_accessed=4 << 20, transcendentals=0
         ),
         name="chi_tiles",
-    )(meta, *tiles, received, three_center)
-
-    pair_sum = keep + lax.ppermute(give, "c", swap)
+    )(meta, kept_tiles, moved_tiles, received, three_center)
+
+    pair_sum = keep + lax.ppermute(give, "c", flip)
     gathered = lax.all_to_all(
         pair_sum.astype(bf16).reshape(128, 8, 128),
-        ("zl", "x", "y", "zh"),
+        ZX + ("y", "zh"),
         split_axis=0,
         concat_axis=0,
         tiled=True,
@@ -322,7 +351,7 @@
 
 
 def solution(mesh):
-    fine = Mesh(mesh.devices.reshape(4, 4, 2, 4, 2), ALL)
+    fine = Mesh(mesh.devices.reshape(2, 2, 4, 2, 4, 2), ALL)
     return jax.shard_map(
         body,
         mesh=fine,
@@ -337,6 +366,6 @@
             P(ALL, None),
             P(ALL, None, None),
         ),
-        out_specs=P(("zl", "x", "c"), ("y", "zh")),
+        out_specs=P(ZX + ("c",), ("y", "zh")),
         check_vma=False,
     )

time: 176 us -> 174 us (0.989)
  waiting for transfers between devices: 83.1 us -> 59.7 us
  starting transfers between devices: 28.6 us -> 37.7 us
  local copies, waits for them, and re-layouts: 5.35 us -> 13.4 us
  other arithmetic: 1.26 us -> 7.69 us
  Pallas kernels: 30.1 us -> 28.2 us
    all_to_all x2, waiting for transfers between devices: 57.6 us -> 4.65 us  [the longest x1 4.64 us: body(): mine = spread_out(payload_call(occ_coef, vir_coef, extra), ZX)]
    ppermute x7 -> x6, waiting for transfers between devices: 23.6 us -> 45.7 us  [shift(): lax.ppermute(rows, axis, [(i, (i + k) % size) for i in range(size)])]
    ppermute x2 -> x5, starting transfers between devices: 0.1 us -> 12.7 us  [the longest x1 12.3 us: body(): lax.ppermute((summed[1] + crossed[1]).astype(bf16), 'zb', flip)]
    ppermute x2 -> x5, waiting for transfers between devices: 1.9 us -> 9.33 us  [the longest x1 5.73 us: body(): crossed = lax.ppermute(summed[2:].astype(bf16), 'za', flip).astype(f32)]
    slice x2 -> x3, local copies, waits for them, and re-layouts: 0.03 us -> 4.01 us  [the longest x1 1.99 us: body(): kept[k]]
    ppermute x7 -> x6, starting transfers between devices: 12.7 us -> 9.19 us  [shift(): lax.ppermute(rows, axis, [(i, (i + k) % size) for i in range(size)])]
    another operation x1 -> x4, other arithmetic: 0.16 us -> 3.66 us  [the longest x3 2.58 us: body(): jnp.stack([kept[k], given[k]])]
    gather x1 -> x4, local copies, waits for them, and re-layouts: 2.05 us -> 4.52 us  [the longest x2 2.27 us: body(): kept = three_center[sends[(to_row + c).reshape(-1)]]]
  transfers between devices with their start and end apart: 11 -> 13, of which waited for: 8 -> 8; matrix products, arithmetic and copies ran while one was open for 3% -> 12% of each run, Pallas kernels for 10% -> 9%
where the time goes in v3:
time: 174 us; the launch traced here: 173 us
  waiting for transfers between devices  59.7 us (34%)
  starting transfers between devices  37.7 us (22%)
  Pallas kernels  28.2 us (16%)
  blocking collectives  26.5 us (15%)
  local copies, waits for them, and re-layouts  13.4 us (8%)
  other arithmetic  7.69 us (4%)
    ppermute x6, waiting for transfers between devices, shift(): lax.ppermute(rows, axis, [(i, (i + k) % size) for i in range(size)])  45.7 us
    all_to_all x1, blocking collectives, body(): lax.all_to_all(pair_sum.astype(bf16).reshape(128, 8, 128), ZX + ('y', 'zh...  26.5 us
    pallas_call x2, Pallas kernels, dens_call(): pl.pallas_call(functools.partial(dens_kernel, jobs), out_shape=(part,) *...  15.9 us
    ppermute x1, starting transfers between devices, body(): lax.ppermute((summed[1] + crossed[1]).astype(bf16), 'zb', flip)  12.3 us
    ppermute x6, starting transfers between devices, shift(): lax.ppermute(rows, axis, [(i, (i + k) % size) for i in range(size)])  9.19 us
    pallas_call x1, Pallas kernels, body(): pl.pallas_call(tile_kernel, out_shape=(out_half, out_half), in_specs=[sme...  9.04 us
    all_to_all x1, starting transfers between devices, body(): mine = spread_out(payload_call(occ_coef, vir_coef, extra), ZX)  8.63 us
    all_to_all x1, starting transfers between devices, body(): received = spread_out(by_z, ZL)  7.17 us
  transfers between devices with their start and end apart: 13, of which 8 were waited for; matrix products, arithmetic and copies ran while one was open for 12% of the time, Pallas kernels for 9%

profile of v3, /device:TPU:32, one launch (start us, length us, event | category | flops | bytes accessed | tf_op | source)
XLA Modules:
  0.0 173.4 jit_solution(2716544185099303015)
XLA Ops:
  0.0 0.0 copy-start
  0.0 3.3 %coef_payload.1 = bf16[16,680,128]{2,1,0:T(8,128)(2,1)} custom-call(bf16[96,4096]{1,0:T(8,128)(2,1)} %occ.1, bf16[96,10240]{1,0:T(8,128)(2,1)} %vir.1, s32[3,8]{1,0:T(4,128)} %bitcast.62, s32[8,12]{1,0:T(8,128)} %refs_1_.1, s32[3,8,12]{2,1,0:T(8,128)} %bitcast.61), custom_call_target="tpu_custom_call" | custom-call | bytes 6291456 | tf_op jit(solution)/shard_map/coef_payload/pallas_call | solution.py:96
  3.3 0.0 copy-start.1
  3.3 8.6 %all-to-all-start = ((bf16[16,680,128]{2,1,0:T(8,128)(2,1)}), bf16[16,680,128]{2,1,0:T(8,128)(2,1)S(1)}, u32[]{:S(2)}, u32[]{:S(2)}) async-start(bf16[16,680,128]{2,1,0:T(8,128)(2,1)} %coef_payload.1), calls=%async_computation | async-start | bytes 5570560 | tf_op jit(solution)/shard_map/all_to_all | solution.py:276
  11.9 0.1 add_add_fusion.1
  12.0 0.1 sub.36
  12.1 0.0 copy-done
  12.1 0.7 gather_fusion.2
  12.8 1.6 gather_fusion.3
  14.4 0.0 collective-permute-start
  14.4 0.1 add.185
  14.5 0.7 gather_fusion
  15.2 1.6 gather_fusion.1
  16.8 2.0 %slice_bitcast_fusion.7 = (bf16[1,4,128,256]{3,2,1,0:T(8,128)(2,1)}, bf16[1,4,128,256]{3,2,1,0:T(8,128)(2,1)S(1)}, bf16[1,4,128,256]{3,2,1,0:T(8,128)(2,1)S(1)}, bf16[1,4,128,256]{3,2,1,0:T(8,128)(2,1)S(1)}) fusion(bf16[16,128,256]{2,1,0:T(8,128)(2,1)} %gather_fusion.1), kind=kLoop, calls=%fused_computation.21 | loop fusion | bytes 2097152 | tf_op jit(solution)/shard_map/slice | solution.py:286
  18.8 0.0 collective-permute-done
  18.8 2.0 %slice_bitcast_fusion.6 = (bf16[1,4,128,256]{3,2,1,0:T(8,128)(2,1)}, bf16[1,4,128,256]{3,2,1,0:T(8,128)(2,1)S(1)}, bf16[1,4,128,256]{3,2,1,0:T(8,128)(2,1)S(1)}, bf16[1,4,128,256]{3,2,1,0:T(8,128)(2,1)S(1)}) fusion(bf16[16,128,256]{2,1,0:T(8,128)(2,1)} %collective-permute-done), kind=kLoop, calls=%fused_computation.20 | loop fusion | bytes 2097152 | tf_op jit(solution)/shard_map/slice | solution.py:286
  20.8 0.9 pad_maximum_fusion
  21.6 1.5 collective-permute-start.1
  23.1 0.9 pad_maximum_fusion.1
  24.0 2.7 %collective-permute-start.2 = (bf16[2,4,128,256]{3,2,1,0:T(8,128)(2,1)}, bf16[2,4,128,256]{3,2,1,0:T(8,128)(2,1)}, u32[]{:S(2)}, u32[]{:S(2)}) collective-permute-start(bf16[2,4,128,256]{3,2,1,0:T(8,128)(2,1)} %pad_maximum_fusion.1), channel_id=1, source_target_pairs={{0,32},{16,48},{32,0},{48,16},{1,33},{17,49},{33,1},{49,17},{2,34}... | collective-permute-start | bytes 1572872 | tf_op jit(solution)/shard_map/ppermute | solution.py:255
  26.6 0.8 pad_maximum_fusion.2
  27.5 1.5 collective-permute-start.3
  29.0 0.8 dynamic_slice.6
  29.7 0.8 dynamic_slice.7
  30.5 0.1 pad_add_fusion.pos
  30.6 1.1 maximum_bitcast_fusion.1
  31.6 19.1 %collective-permute-done.1 = bf16[2,4,128,256]{3,2,1,0:T(8,128)(2,1)} collective-permute-done((bf16[2,4,128,256]{3,2,1,0:T(8,128)(2,1)}, bf16[2,4,128,256]{3,2,1,0:T(8,128)(2,1)}, u32[]{:S(2)}, u32[]{:S(2)}) %collective-permute-start.1) | collective-permute-done | bytes 524320 | tf_op jit(solution)/shard_map/ppermute | solution.py:255
  50.7 15.1 %collective-permute-done.2 = bf16[2,4,128,256]{3,2,1,0:T(8,128)(2,1)} collective-permute-done((bf16[2,4,128,256]{3,2,1,0:T(8,128)(2,1)}, bf16[2,4,128,256]{3,2,1,0:T(8,128)(2,1)}, u32[]{:S(2)}, u32[]{:S(2)}) %collective-permute-start.2) | collective-permute-done | bytes 524320 | tf_op jit(solution)/shard_map/ppermute | solution.py:255
  65.8 0.0 collective-permute-done.3
  65.8 1.6 maximum_bitcast_fusion
  67.5 1.5 copy.11
  69.0 4.6 %all-to-all-done.mine = bf16[16,680,128]{2,1,0:T(8,128)(2,1)S(1)} async-done(((bf16[16,680,128]{2,1,0:T(8,128)(2,1)}), bf16[16,680,128]{2,1,0:T(8,128)(2,1)S(1)}, u32[]{:S(2)}, u32[]{:S(2)}) %all-to-all-start) | async-done | bytes 2785312 | tf_op jit(solution)/shard_map/all_to_all | solution.py:276
  73.6 0.0 collective-permute-start.4
  73.6 7.2 %all-to-all-start.1 = ((bf16[32,128,256]{2,1,0:T(8,128)(2,1)}), bf16[32,128,256]{2,1,0:T(8,128)(2,1)}, u32[]{:S(2)}, u32[]{:S(2)}) async-start(bf16[32,128,256]{2,1,0:T(8,128)(2,1)} %bitcast.59), calls=%async_computation.1 | async-start | bytes 4194304 | tf_op jit(solution)/shard_map/all_to_all | solution.py:296
  80.8 0.0 collective-permute-done.4.other
  80.8 4.8 %density_partials.3 = bf16[4,384,128]{2,1,0:T(8,128)(2,1)S(1)} custom-call(s32[128,128]{1,0:T(8,128)S(1)} %bitcast_convert_fusion.tab, s32[4]{0:T(128)S(1)} %pad_add_fusion.pos, bf16[16,680,128]{2,1,0:T(8,128)(2,1)S(1)} %all-to-all-done.mine, bf16[16,680,128]{2,1,0:T(8,128)(2,1)} %collective-permute-done.4.other, f32[7,128]{1,0:T(8,128)S(1)} %maximum_bitcast_fusion.2.wts), custom_call_target="tpu_custom_call" | custom-call | flops 469762048 | bytes 6291456 | tf_op jit(solution)/shard_map/density_partials/pallas_call | solution.py:181
  85.6 0.0 copy-start.3
  85.6 0.6 collective-permute-start.5
  86.2 11.1 %density_partials.2 = (bf16[4,384,128]{2,1,0:T(8,128)(2,1)S(1)}, bf16[4,384,128]{2,1,0:T(8,128)(2,1)}, bf16[4,384,128]{2,1,0:T(8,128)(2,1)S(1)}) custom-call(s32[128,128]{1,0:T(8,128)S(1)} %bitcast_convert_fusion.tab, s32[4]{0:T(128)S(1)} %pad_add_fusion.pos, bf16[16,680,128]{2,1,0:T(8,128)(2,1)S(1)} %all-to-all-done.mine, ...), custom_call_target="tpu_custom_call" | custom-call | flops 1409286144 | bytes 6291456 | tf_op jit(solution)/shard_map/density_partials/pallas_call | solution.py:181
  97.3 2.9 %collective-permute-start.7 = (bf16[4,384,128]{2,1,0:T(8,128)(2,1)}, bf16[4,384,128]{2,1,0:T(8,128)(2,1)S(1)}, u32[]{:S(2)}, u32[]{:S(2)}) collective-permute-start(bf16[4,384,128]{2,1,0:T(8,128)(2,1)} %get-tuple-element.19), channel_id=1, source_target_pairs={{0,48},{16,0},{32,16},{48,32},{1,49},{17,1},{33,17},{49,33},{2,50}... | collective-permute-start | bytes 1179656 | tf_op jit(solution)/shard_map/ppermute | solution.py:255
  100.2 0.0 collective-permute-done.5
  100.2 0.1 add_convert_fusion
  100.4 0.1 collective-permute-start.6
  100.5 0.1 reshape.152
  100.5 8.2 %collective-permute-done.7 = bf16[4,384,128]{2,1,0:T(8,128)(2,1)S(1)} collective-permute-done((bf16[4,384,128]{2,1,0:T(8,128)(2,1)}, bf16[4,384,128]{2,1,0:T(8,128)(2,1)S(1)}, u32[]{:S(2)}, u32[]{:S(2)}) %collective-permute-start.7) | collective-permute-done | bytes 393248 | tf_op jit(solution)/shard_map/ppermute | solution.py:255
  108.7 3.3 %collective-permute-done.6 = bf16[4,384,128]{2,1,0:T(8,128)(2,1)S(1)} collective-permute-done((bf16[4,384,128]{2,1,0:T(8,128)(2,1)S(1)}, bf16[4,384,128]{2,1,0:T(8,128)(2,1)S(1)}, u32[]{:S(2)}, u32[]{:S(2)}) %collective-permute-start.6) | collective-permute-done | bytes 393248 | tf_op jit(solution)/shard_map/ppermute | solution.py:255
  112.0 1.2 convert_add_fusion
  113.2 0.4 collective-permute-start.8
  113.6 0.7 slice_bitcast_fusion.8
  114.3 5.7 %collective-permute-done.8 = bf16[2,384,128]{2,1,0:T(8,128)(2,1)S(1)} collective-permute-done((bf16[2,384,128]{2,1,0:T(8,128)(2,1)S(1)}, bf16[2,384,128]{2,1,0:T(8,128)(2,1)S(1)}, u32[]{:S(2)}, u32[]{:S(2)}) %collective-permute-start.8) | collective-permute-done | bytes 196640 | tf_op jit(solution)/shard_map/ppermute | solution.py:306
  120.1 12.3 %collective-permute-start.9 = (bf16[384,128]{1,0:T(8,128)(2,1)S(1)}, bf16[384,128]{1,0:T(8,128)(2,1)S(1)}, u32[]{:S(2)}, u32[]{:S(2)}) collective-permute-start(bf16[384,128]{1,0:T(8,128)(2,1)S(1)} %get-tuple-element.23), channel_id=1, source_target_pairs={{0,128},{128,0},{1,129},{129,1},{2,130},{130,2},{3,131},{131,3},{4... | collective-permute-start | bytes 294920 | tf_op jit(solution)/shard_map/ppermute | solution.py:308
  132.4 0.7 slice.79
  133.1 0.1 reshape_squeeze.3
  133.2 0.1 concatenate.9.meta
  133.3 0.0 all-to-all-done.1.blocks
  133.3 1.7 collective-permute-done.9.moved
  135.0 9.0 %chi_tiles.1 = (f32[16,8,8,128]{3,2,1,0:T(8,128)S(1)}, f32[16,8,8,128]{3,2,1,0:T(8,128)S(1)}) custom-call(s32[256]{0:T(256)S(1)} %concatenate.9.meta, f32[384,128]{1,0:T(8,128)S(1)} %get-tuple-element.24.kept, bf16[384,128]{1,0:T(8,128)(2,1)S(1)} %collective-permute-done.9.moved, bf16[32,128,256]{2,1,0:T(8,128)(2,1)} %all-to-all-done.1.blocks, ...), custom_call_target="tpu_custom_call" | custom-call | flops 1610612736 | bytes 4194304 | tf_op jit(solution)/shard_map/chi_tiles/pallas_call | solution.py:319
  144.0 0.1 collective-permute-start.10
  144.1 1.9 %collective-permute-done.10 = f32[16,8,8,128]{3,2,1,0:T(8,128)S(1)} collective-permute-done((f32[16,8,8,128]{3,2,1,0:T(8,128)S(1)}, f32[16,8,8,128]{3,2,1,0:T(8,128)S(1)}, u32[]{:S(2)}, u32[]{:S(2)}) %collective-permute-start.10) | collective-permute-done | bytes 524320 | tf_op jit(solution)/shard_map/ppermute | solution.py:341
  146.0 0.1 add_convert_fusion.1
  146.1 26.5 %all_to_all.15 = bf16[128,8,128]{2,1,0:T(8,128)(2,1)S(1)} all-to-all(bf16[128,8,128]{2,1,0:T(8,128)(2,1)S(1)} %bitcast.60), channel_id=1, replica_groups=mesh['zb'=2,'za'=2,'x'=4,'c'=2,'y'=4,'zh'=2] {'zb','za','x','y','zh'}, dimensions={0} | all-to-all | bytes 524288 | tf_op jit(solution)/shard_map/all_to_all | solution.py:342
  172.6 0.1 convert_reduce_fusion
  172.7 0.1 fusion.16
  172.8 0.6 pad_maximum_fusion.3
  (22 shorter events, 0.2 us)
Async XLA Ops:
  0.0 12.1 %copy-start = (s32[32,1]{0,1:T(1,128)S(1)}, s32[32,1]{0,1:T(1,128)}, u32[]{:S(2)}) copy-start(s32[32,1]{0,1:T(1,128)} %param.15) | copy-start | bytes 388
  3.3 9.5 %copy-start.1 = (bf16[8,128,256]{2,1,0:T(8,128)(2,1)S(1)}, bf16[8,128,256]{2,1,0:T(8,128)(2,1)}, u32[]{:S(2)}) copy-start(bf16[8,128,256]{2,1,0:T(8,128)(2,1)} %own.1) | copy-start | bytes 1572868
  3.3 70.3 %all-to-all-start = ((bf16[16,680,128]{2,1,0:T(8,128)(2,1)}), bf16[16,680,128]{2,1,0:T(8,128)(2,1)S(1)}, u32[]{:S(2)}, u32[]{:S(2)}) async-start(bf16[16,680,128]{2,1,0:T(8,128)(2,1)} %coef_payload.1), calls=%async_computation | async-start | bytes 5570560 | tf_op jit(solution)/shard_map/all_to_all | solution.py:276
  14.4 4.4 %collective-permute-start = (bf16[16,128,256]{2,1,0:T(8,128)(2,1)}, bf16[16,128,256]{2,1,0:T(8,128)(2,1)}, u32[]{:S(2)}, u32[]{:S(2)}) collective-permute-start(bf16[16,128,256]{2,1,0:T(8,128)(2,1)} %gather_fusion.3), channel_id=1, source_target_pairs={{0,8},{8,0},{1,9},{9,1},{2,10},{10,2},{3,11},{11,3},{4,12},{12,4},... | collective-permute-start | bytes 3145736 | tf_op jit(solution)/shard_map/ppermute | solution.py:283
  21.6 29.1 %collective-permute-start.1 = (bf16[2,4,128,256]{3,2,1,0:T(8,128)(2,1)}, bf16[2,4,128,256]{3,2,1,0:T(8,128)(2,1)}, u32[]{:S(2)}, u32[]{:S(2)}) collective-permute-start(bf16[2,4,128,256]{3,2,1,0:T(8,128)(2,1)} %pad_maximum_fusion), channel_id=1, source_target_pairs={{0,16},{16,32},{32,48},{48,0},{1,17},{17,33},{33,49},{49,1},{2,18}... | collective-permute-start | bytes 1572872 | tf_op jit(solution)/shard_map/ppermute | solution.py:255
  24.0 41.9 %collective-permute-start.2 = (bf16[2,4,128,256]{3,2,1,0:T(8,128)(2,1)}, bf16[2,4,128,256]{3,2,1,0:T(8,128)(2,1)}, u32[]{:S(2)}, u32[]{:S(2)}) collective-permute-start(bf16[2,4,128,256]{3,2,1,0:T(8,128)(2,1)} %pad_maximum_fusion.1), channel_id=1, source_target_pairs={{0,32},{16,48},{32,0},{48,16},{1,33},{17,49},{33,1},{49,17},{2,34}... | collective-permute-start | bytes 1572872 | tf_op jit(solution)/shard_map/ppermute | solution.py:255
  27.5 38.4 %collective-permute-start.3 = (bf16[2,4,128,256]{3,2,1,0:T(8,128)(2,1)}, bf16[2,4,128,256]{3,2,1,0:T(8,128)(2,1)}, u32[]{:S(2)}, u32[]{:S(2)}) collective-permute-start(bf16[2,4,128,256]{3,2,1,0:T(8,128)(2,1)} %pad_maximum_fusion.2), channel_id=1, source_target_pairs={{0,48},{16,0},{32,16},{48,32},{1,49},{17,1},{33,17},{49,33},{2,50}... | collective-permute-start | bytes 1572872 | tf_op jit(solution)/shard_map/ppermute | solution.py:255
  73.6 7.2 %collective-permute-start.4 = (bf16[16,680,128]{2,1,0:T(8,128)(2,1)S(1)}, bf16[16,680,128]{2,1,0:T(8,128)(2,1)}, u32[]{:S(2)}, u32[]{:S(2)}) collective-permute-start(bf16[16,680,128]{2,1,0:T(8,128)(2,1)S(1)} %all-to-all-done.mine), channel_id=1, source_target_pairs={{0,8},{8,0},{1,9},{9,1},{2,10},{10,2},{3,11},{11,3},{4,12},{12,4},... | collective-permute-start | bytes 8355848 | tf_op jit(solution)/shard_map/ppermute | solution.py:298
  73.6 59.7 %all-to-all-start.1 = ((bf16[32,128,256]{2,1,0:T(8,128)(2,1)}), bf16[32,128,256]{2,1,0:T(8,128)(2,1)}, u32[]{:S(2)}, u32[]{:S(2)}) async-start(bf16[32,128,256]{2,1,0:T(8,128)(2,1)} %bitcast.59), calls=%async_computation.1 | async-start | bytes 4194304 | tf_op jit(solution)/shard_map/all_to_all | solution.py:296
  85.6 14.9 %copy-start.3 = (s32[8,12]{1,0:T(8,128)S(1)}, s32[8,12]{1,0:T(8,128)}, u32[]{:S(2)}) copy-start(s32[8,12]{1,0:T(8,128)} %refs_1_.1) | copy-start | bytes 1156
  85.6 14.6 %collective-permute-start.5 = (bf16[4,384,128]{2,1,0:T(8,128)(2,1)S(1)}, bf16[4,384,128]{2,1,0:T(8,128)(2,1)S(1)}, u32[]{:S(2)}, u32[]{:S(2)}) collective-permute-start(bf16[4,384,128]{2,1,0:T(8,128)(2,1)S(1)} %density_partials.3), channel_id=1, source_target_pairs={{0,16},{16,32},{32,48},{48,0},{1,17},{17,33},{33,49},{49,1},{2,18}... | collective-permute-start | bytes 1179656 | tf_op jit(solution)/shard_map/ppermute | solution.py:255
  97.3 3.1 %copy-start.2 = (bf16[4,384,128]{2,1,0:T(8,128)(2,1)}, bf16[4,384,128]{2,1,0:T(8,128)(2,1)S(1)}, u32[]{:S(2)}) copy-start(bf16[4,384,128]{2,1,0:T(8,128)(2,1)S(1)} %get-tuple-element.17) | copy-start | bytes 1179652
  97.3 11.4 %collective-permute-start.7 = (bf16[4,384,128]{2,1,0:T(8,128)(2,1)}, bf16[4,384,128]{2,1,0:T(8,128)(2,1)S(1)}, u32[]{:S(2)}, u32[]{:S(2)}) collective-permute-start(bf16[4,384,128]{2,1,0:T(8,128)(2,1)} %get-tuple-element.19), channel_id=1, source_target_pairs={{0,48},{16,0},{32,16},{48,32},{1,49},{17,1},{33,17},{49,33},{2,50}... | collective-permute-start | bytes 1179656 | tf_op jit(solution)/shard_map/ppermute | solution.py:255
  100.4 11.7 %collective-permute-start.6 = (bf16[4,384,128]{2,1,0:T(8,128)(2,1)S(1)}, bf16[4,384,128]{2,1,0:T(8,128)(2,1)S(1)}, u32[]{:S(2)}, u32[]{:S(2)}) collective-permute-start(bf16[4,384,128]{2,1,0:T(8,128)(2,1)S(1)} %add_convert_fusion), channel_id=1, source_target_pairs={{0,16},{16,32},{32,48},{48,0},{1,17},{17,33},{33,49},{49,1},{2,18}... | collective-permute-start | bytes 1179656 | tf_op jit(solution)/shard_map/ppermute | solution.py:255
  113.2 6.8 %collective-permute-start.8 = (bf16[2,384,128]{2,1,0:T(8,128)(2,1)S(1)}, bf16[2,384,128]{2,1,0:T(8,128)(2,1)S(1)}, u32[]{:S(2)}, u32[]{:S(2)}) collective-permute-start(bf16[2,384,128]{2,1,0:T(8,128)(2,1)S(1)} %slice.149), channel_id=1, source_target_pairs={{0,64},{64,0},{1,65},{65,1},{2,66},{66,2},{3,67},{67,3},{4,68},{68... | collective-permute-start | bytes 589832 | tf_op jit(solution)/shard_map/ppermute | solution.py:306
  120.1 14.8 %collective-permute-start.9 = (bf16[384,128]{1,0:T(8,128)(2,1)S(1)}, bf16[384,128]{1,0:T(8,128)(2,1)S(1)}, u32[]{:S(2)}, u32[]{:S(2)}) collective-permute-start(bf16[384,128]{1,0:T(8,128)(2,1)S(1)} %get-tuple-element.23), channel_id=1, source_target_pairs={{0,128},{128,0},{1,129},{129,1},{2,130},{130,2},{3,131},{131,3},{4... | collective-permute-start | bytes 294920 | tf_op jit(solution)/shard_map/ppermute | solution.py:308
  144.0 2.0 %collective-permute-start.10 = (f32[16,8,8,128]{3,2,1,0:T(8,128)S(1)}, f32[16,8,8,128]{3,2,1,0:T(8,128)S(1)}, u32[]{:S(2)}, u32[]{:S(2)}) collective-permute-start(f32[16,8,8,128]{3,2,1,0:T(8,128)S(1)} %get-tuple-element.22), channel_id=1, source_target_pairs={{0,8},{8,0},{1,9},{9,1},{2,10},{10,2},{3,11},{11,3},{4,12},{12,4},... | collective-permute-start | bytes 1572872 | tf_op jit(solution)/shard_map/ppermute | solution.py:341

commit v4 on v3

--- a/solution.py
+++ b/solution.py
@@ -200,8 +200,9 @@
 
 
 def tile_kernel(
-    meta, kept, moved, blocks, own, keep, give, recv, dens, occ_exp, vir_exp, kron, acc, chi, sem
+    meta, kept, moved, blocks, own, keep, give, recv, dens, *refs
 ):
+    occs, virs, krons, accs, (chi, sem) = refs[0:4], refs[4:8], refs[8:12], refs[12:16], refs[16:]
     load = pltpu.make_async_copy(blocks, recv, sem)
     load.start()
     dens[...] = (kept[...] + moved[...].astype(f32)).astype(bf16)
@@ -211,30 +212,41 @@
 
     load.wait()
 
-    def per_pair(j, carry):
+    def expand(j, occ_exp, vir_exp, acc):
         hot_occ = (row == j * BB + col // BB).astype(f32).astype(bf16)
         hot_vir = (row == j * BB + col % BB).astype(f32).astype(bf16)
         occ_exp[...] = jnp.dot(dens[0:TR, :], hot_occ, preferred_element_type=f32)
         vir_exp[...] = jnp.dot(dens[TR : 2 * TR, :], hot_vir, preferred_element_type=f32)
         acc[...] = jnp.zeros_like(acc)
-        for t in range(NNB):
-            buf = t % 2
-            vir = vir_exp[t * BB : (t + 1) * BB, :].astype(bf16)
-            for lam in range(BB):
-                occ = jnp.broadcast_to(occ_exp[t * BB + lam : t * BB + lam + 1, :], (BB, BB * BB))
-                kron[buf, lam * BB : (lam + 1) * BB, :] = occ.astype(bf16) * vir
-            slot = meta[j * NNB + t]
-            aux = meta[128 + j * NNB + t]
-            paired = jnp.dot(recv[slot], kron[buf], preferred_element_type=f32)
-            acc[aux] = acc[aux] + paired
+
+    def add_partner(j, t, occ_exp, vir_exp, kron, acc):
+        buf = t % 2
+        vir = vir_exp[t * BB : (t + 1) * BB, :].astype(bf16)
+        for lam in range(BB):
+            occ = jnp.broadcast_to(occ_exp[t * BB + lam : t * BB + lam + 1, :], (BB, BB * BB))
+            kron[buf, lam * BB : (lam + 1) * BB, :] = occ.astype(bf16) * vir
+        slot = meta[j * NNB + t]
+        aux = meta[128 + j * NNB + t]
+        acc[aux] = acc[aux] + jnp.dot(recv[slot], kron[buf], preferred_element_type=f32)
+
+    def finish(j, acc):
         target = meta[240 + j]
         rows = acc[...].reshape(NAB * AB, BB * BB).astype(bf16)
         chi[target] += lax.dot_general(
             own[j], rows, (((1,), (1,)), ((), ())), preferred_element_type=f32
         )
+
+    def per_four(i, carry):
+        for n in range(4):
+            expand(4 * i + n, occs[n], virs[n], accs[n])
+        for t in range(NNB):
+            for n in range(4):
+                add_partner(4 * i + n, t, occs[n], virs[n], krons[n], accs[n])
+        for n in range(4):
+            finish(4 * i + n, accs[n])
         return carry
 
-    lax.fori_loop(0, NJ, per_pair, 0)
+    lax.fori_loop(0, NJ // 4, per_four, 0)
     low = lax.broadcasted_iota(jnp.int32, (1, 8, 128), 2) < 64
     first = jnp.full((1, 8, 128), meta[248], jnp.int32) == 0
     for tile in range(4):
@@ -324,13 +336,11 @@
         scratch_shapes=[
             pltpu.VMEM((32, AB, BB * BB), bf16),
             pltpu.VMEM((2 * TR, NJ * BB), bf16),
-            pltpu.VMEM((TR, BB * BB), f32),
-            pltpu.VMEM((TR, BB * BB), f32),
-            pltpu.VMEM((2, BB * BB, BB * BB), bf16),
-            pltpu.VMEM((NAB, AB, BB * BB), f32),
-            pltpu.VMEM((NAB, AB, NAB * AB), f32),
-            pltpu.SemaphoreType.DMA,
-        ],
+        ]
+        + [pltpu.VMEM((TR, BB * BB), f32)] * 8
+        + [pltpu.VMEM((2, BB * BB, BB * BB), bf16)] * 4
+        + [pltpu.VMEM((NAB, AB, BB * BB), f32)] * 4
+        + [pltpu.VMEM((NAB, AB, NAB * AB), f32), pltpu.SemaphoreType.DMA],
         compiler_params=pltpu.CompilerParams(vmem_limit_bytes=32 << 20),
         cost_estimate=pl.CostEstimate(
             flops=2 * 96 * 128 * 256 * 256, bytes_accessed=4 << 20, transcendentals=0

time: 174 us -> 171 us (0.983)
  Pallas kernels: 28.2 us -> 25.6 us
    pallas_call x1, Pallas kernels: 9.04 us -> 6.46 us  [body(): pl.pallas_call(tile_kernel, out_shape=(out_half, out_half), in_specs=[sme...]
where the time goes in v4:
time: 171 us
  waiting for transfers between devices  59.7 us (35%)
  starting transfers between devices  37.7 us (22%)
  blocking collectives  26.4 us (15%)
  Pallas kernels  25.6 us (15%)
  local copies, waits for them, and re-layouts  13.4 us (8%)
  other arithmetic  7.69 us (4%)
    ppermute x6, waiting for transfers between devices, shift(): lax.ppermute(rows, axis, [(i, (i + k) % size) for i in range(size)])  45.7 us
    all_to_all x1, blocking collectives, body(): lax.all_to_all(pair_sum.astype(bf16).reshape(128, 8, 128), ZX + ('y', 'zh...  26.4 us
    pallas_call x2, Pallas kernels, dens_call(): pl.pallas_call(functools.partial(dens_kernel, jobs), out_shape=(part,) *...  15.9 us
    ppermute x1, starting transfers between devices, body(): lax.ppermute((summed[1] + crossed[1]).astype(bf16), 'zb', flip)  12.3 us
    ppermute x6, starting transfers between devices, shift(): lax.ppermute(rows, axis, [(i, (i + k) % size) for i in range(size)])  9.19 us
    all_to_all x1, starting transfers between devices, body(): mine = spread_out(payload_call(occ_coef, vir_coef, extra), ZX)  8.63 us
    all_to_all x1, starting transfers between devices, body(): received = spread_out(by_z, ZL)  7.17 us
    pallas_call x1, Pallas kernels, body(): pl.pallas_call(tile_kernel, out_shape=(out_half, out_half), in_specs=[sme...  6.46 us
  transfers between devices with their start and end apart: 13, of which 8 were waited for; matrix products, arithmetic and copies ran while one was open for 12% of the time, Pallas kernels for 9%

profile of v4, /device:TPU:32, one launch (start us, length us, event | category | flops | bytes accessed | tf_op | source)
XLA Modules:
  0.0 170.8 jit_solution(16485856977685650198)
XLA Ops:
  0.0 3.3 %coef_payload.1 = bf16[16,680,128]{2,1,0:T(8,128)(2,1)} custom-call(bf16[96,4096]{1,0:T(8,128)(2,1)} %occ.1, bf16[96,10240]{1,0:T(8,128)(2,1)} %vir.1, s32[3,8]{1,0:T(4,128)} %bitcast.62, s32[8,12]{1,0:T(8,128)} %refs_1_.1, s32[3,8,12]{2,1,0:T(8,128)} %bitcast.61), custom_call_target="tpu_custom_call" | custom-call | bytes 6291456 | tf_op jit(solution)/shard_map/coef_payload/pallas_call | solution.py:96
  3.3 0.0 copy-start.1
  3.3 8.6 %all-to-all-start = ((bf16[16,680,128]{2,1,0:T(8,128)(2,1)}), bf16[16,680,128]{2,1,0:T(8,128)(2,1)S(1)}, u32[]{:S(2)}, u32[]{:S(2)}) async-start(bf16[16,680,128]{2,1,0:T(8,128)(2,1)} %coef_payload.1), calls=%async_computation | async-start | bytes 5570560 | tf_op jit(solution)/shard_map/all_to_all | solution.py:288
  11.9 0.1 add_add_fusion.1
  12.0 0.1 sub.36
  12.1 0.0 copy-done
  12.1 0.7 gather_fusion.2
  12.8 1.6 gather_fusion.3
  14.4 0.0 collective-permute-start
  14.4 0.1 add.185
  14.5 0.7 gather_fusion
  15.2 1.6 gather_fusion.1
  16.8 2.0 %slice_bitcast_fusion.7 = (bf16[1,4,128,256]{3,2,1,0:T(8,128)(2,1)}, bf16[1,4,128,256]{3,2,1,0:T(8,128)(2,1)S(1)}, bf16[1,4,128,256]{3,2,1,0:T(8,128)(2,1)S(1)}, bf16[1,4,128,256]{3,2,1,0:T(8,128)(2,1)S(1)}) fusion(bf16[16,128,256]{2,1,0:T(8,128)(2,1)} %gather_fusion.1), kind=kLoop, calls=%fused_computation.21 | loop fusion | bytes 2097152 | tf_op jit(solution)/shard_map/slice | solution.py:298
  18.8 0.0 collective-permute-done
  18.8 2.0 %slice_bitcast_fusion.6 = (bf16[1,4,128,256]{3,2,1,0:T(8,128)(2,1)}, bf16[1,4,128,256]{3,2,1,0:T(8,128)(2,1)S(1)}, bf16[1,4,128,256]{3,2,1,0:T(8,128)(2,1)S(1)}, bf16[1,4,128,256]{3,2,1,0:T(8,128)(2,1)S(1)}) fusion(bf16[16,128,256]{2,1,0:T(8,128)(2,1)} %collective-permute-done), kind=kLoop, calls=%fused_computation.20 | loop fusion | bytes 2097152 | tf_op jit(solution)/shard_map/slice | solution.py:298
  20.8 0.9 pad_maximum_fusion
  21.6 1.5 collective-permute-start.1
  23.1 0.9 pad_maximum_fusion.1
  24.0 2.7 %collective-permute-start.2 = (bf16[2,4,128,256]{3,2,1,0:T(8,128)(2,1)}, bf16[2,4,128,256]{3,2,1,0:T(8,128)(2,1)}, u32[]{:S(2)}, u32[]{:S(2)}) collective-permute-start(bf16[2,4,128,256]{3,2,1,0:T(8,128)(2,1)} %pad_maximum_fusion.1), channel_id=1, source_target_pairs={{0,32},{16,48},{32,0},{48,16},{1,33},{17,49},{33,1},{49,17},{2,34}... | collective-permute-start | bytes 1572872 | tf_op jit(solution)/shard_map/ppermute | solution.py:267
  26.6 0.8 pad_maximum_fusion.2
  27.5 1.5 collective-permute-start.3
  29.0 0.8 dynamic_slice.6
  29.7 0.8 dynamic_slice.7
  30.5 0.1 pad_add_fusion.pos
  30.6 1.1 maximum_bitcast_fusion.1
  31.6 19.1 %collective-permute-done.1 = bf16[2,4,128,256]{3,2,1,0:T(8,128)(2,1)} collective-permute-done((bf16[2,4,128,256]{3,2,1,0:T(8,128)(2,1)}, bf16[2,4,128,256]{3,2,1,0:T(8,128)(2,1)}, u32[]{:S(2)}, u32[]{:S(2)}) %collective-permute-start.1) | collective-permute-done | bytes 524320 | tf_op jit(solution)/shard_map/ppermute | solution.py:267
  50.7 15.1 %collective-permute-done.2 = bf16[2,4,128,256]{3,2,1,0:T(8,128)(2,1)} collective-permute-done((bf16[2,4,128,256]{3,2,1,0:T(8,128)(2,1)}, bf16[2,4,128,256]{3,2,1,0:T(8,128)(2,1)}, u32[]{:S(2)}, u32[]{:S(2)}) %collective-permute-start.2) | collective-permute-done | bytes 524320 | tf_op jit(solution)/shard_map/ppermute | solution.py:267
  65.8 0.0 collective-permute-done.3
  65.8 1.6 maximum_bitcast_fusion
  67.5 1.5 copy.11
  69.0 4.6 %all-to-all-done.mine = bf16[16,680,128]{2,1,0:T(8,128)(2,1)S(1)} async-done(((bf16[16,680,128]{2,1,0:T(8,128)(2,1)}), bf16[16,680,128]{2,1,0:T(8,128)(2,1)S(1)}, u32[]{:S(2)}, u32[]{:S(2)}) %all-to-all-start) | async-done | bytes 2785312 | tf_op jit(solution)/shard_map/all_to_all | solution.py:288
  73.6 0.0 collective-permute-start.4
  73.6 7.2 %all-to-all-start.1 = ((bf16[32,128,256]{2,1,0:T(8,128)(2,1)}), bf16[32,128,256]{2,1,0:T(8,128)(2,1)}, u32[]{:S(2)}, u32[]{:S(2)}) async-start(bf16[32,128,256]{2,1,0:T(8,128)(2,1)} %bitcast.59), calls=%async_computation.1 | async-start | bytes 4194304 | tf_op jit(solution)/shard_map/all_to_all | solution.py:308
  80.8 0.0 collective-permute-done.4.other
  80.8 4.8 %density_partials.3 = bf16[4,384,128]{2,1,0:T(8,128)(2,1)S(1)} custom-call(s32[128,128]{1,0:T(8,128)S(1)} %bitcast_convert_fusion.tab, s32[4]{0:T(128)S(1)} %pad_add_fusion.pos, bf16[16,680,128]{2,1,0:T(8,128)(2,1)S(1)} %all-to-all-done.mine, bf16[16,680,128]{2,1,0:T(8,128)(2,1)} %collective-permute-done.4.other, f32[7,128]{1,0:T(8,128)S(1)} %maximum_bitcast_fusion.2.wts), custom_call_target="tpu_custom_call" | custom-call | flops 469762048 | bytes 6291456 | tf_op jit(solution)/shard_map/density_partials/pallas_call | solution.py:181
  85.6 0.0 copy-start.3
  85.6 0.6 collective-permute-start.5
  86.1 11.1 %density_partials.2 = (bf16[4,384,128]{2,1,0:T(8,128)(2,1)S(1)}, bf16[4,384,128]{2,1,0:T(8,128)(2,1)}, bf16[4,384,128]{2,1,0:T(8,128)(2,1)S(1)}) custom-call(s32[128,128]{1,0:T(8,128)S(1)} %bitcast_convert_fusion.tab, s32[4]{0:T(128)S(1)} %pad_add_fusion.pos, bf16[16,680,128]{2,1,0:T(8,128)(2,1)S(1)} %all-to-all-done.mine, ...), custom_call_target="tpu_custom_call" | custom-call | flops 1409286144 | bytes 6291456 | tf_op jit(solution)/shard_map/density_partials/pallas_call | solution.py:181
  97.3 2.9 %collective-permute-start.7 = (bf16[4,384,128]{2,1,0:T(8,128)(2,1)}, bf16[4,384,128]{2,1,0:T(8,128)(2,1)S(1)}, u32[]{:S(2)}, u32[]{:S(2)}) collective-permute-start(bf16[4,384,128]{2,1,0:T(8,128)(2,1)} %get-tuple-element.19), channel_id=1, source_target_pairs={{0,48},{16,0},{32,16},{48,32},{1,49},{17,1},{33,17},{49,33},{2,50}... | collective-permute-start | bytes 1179656 | tf_op jit(solution)/shard_map/ppermute | solution.py:267
  100.2 0.0 collective-permute-done.5
  100.2 0.1 add_convert_fusion
  100.4 0.1 collective-permute-start.6
  100.4 0.0 copy-done.3
  100.5 0.1 reshape.152
  100.5 8.2 %collective-permute-done.7 = bf16[4,384,128]{2,1,0:T(8,128)(2,1)S(1)} collective-permute-done((bf16[4,384,128]{2,1,0:T(8,128)(2,1)}, bf16[4,384,128]{2,1,0:T(8,128)(2,1)S(1)}, u32[]{:S(2)}, u32[]{:S(2)}) %collective-permute-start.7) | collective-permute-done | bytes 393248 | tf_op jit(solution)/shard_map/ppermute | solution.py:267
  108.7 3.3 %collective-permute-done.6 = bf16[4,384,128]{2,1,0:T(8,128)(2,1)S(1)} collective-permute-done((bf16[4,384,128]{2,1,0:T(8,128)(2,1)S(1)}, bf16[4,384,128]{2,1,0:T(8,128)(2,1)S(1)}, u32[]{:S(2)}, u32[]{:S(2)}) %collective-permute-start.6) | collective-permute-done | bytes 393248 | tf_op jit(solution)/shard_map/ppermute | solution.py:267
  112.0 1.2 convert_add_fusion
  113.2 0.4 collective-permute-start.8
  113.6 0.7 slice_bitcast_fusion.8
  114.3 5.8 %collective-permute-done.8 = bf16[2,384,128]{2,1,0:T(8,128)(2,1)S(1)} collective-permute-done((bf16[2,384,128]{2,1,0:T(8,128)(2,1)S(1)}, bf16[2,384,128]{2,1,0:T(8,128)(2,1)S(1)}, u32[]{:S(2)}, u32[]{:S(2)}) %collective-permute-start.8) | collective-permute-done | bytes 196640 | tf_op jit(solution)/shard_map/ppermute | solution.py:318
  120.1 12.3 %collective-permute-start.9 = (bf16[384,128]{1,0:T(8,128)(2,1)S(1)}, bf16[384,128]{1,0:T(8,128)(2,1)S(1)}, u32[]{:S(2)}, u32[]{:S(2)}) collective-permute-start(bf16[384,128]{1,0:T(8,128)(2,1)S(1)} %get-tuple-element.23), channel_id=1, source_target_pairs={{0,128},{128,0},{1,129},{129,1},{2,130},{130,2},{3,131},{131,3},{4... | collective-permute-start | bytes 294920 | tf_op jit(solution)/shard_map/ppermute | solution.py:320
  132.4 0.7 slice.79
  133.1 0.1 reshape_squeeze.3
  133.2 0.1 concatenate.9.meta
  133.3 0.0 all-to-all-done.1.blocks
  133.3 1.7 collective-permute-done.9.moved
  135.0 6.5 %chi_tiles.1 = (f32[16,8,8,128]{3,2,1,0:T(8,128)S(1)}, f32[16,8,8,128]{3,2,1,0:T(8,128)S(1)}) custom-call(s32[256]{0:T(256)S(1)} %concatenate.9.meta, f32[384,128]{1,0:T(8,128)S(1)} %get-tuple-element.24.kept, bf16[384,128]{1,0:T(8,128)(2,1)S(1)} %collective-permute-done.9.moved, bf16[32,128,256]{2,1,0:T(8,128)(2,1)} %all-to-all-done.1.blocks, ...), custom_call_target="tpu_custom_call" | custom-call | flops 1610612736 | bytes 4194304 | tf_op jit(solution)/shard_map/chi_tiles/pallas_call | solution.py:331
  141.4 0.1 collective-permute-start.10
  141.5 1.9 %collective-permute-done.10 = f32[16,8,8,128]{3,2,1,0:T(8,128)S(1)} collective-permute-done((f32[16,8,8,128]{3,2,1,0:T(8,128)S(1)}, f32[16,8,8,128]{3,2,1,0:T(8,128)S(1)}, u32[]{:S(2)}, u32[]{:S(2)}) %collective-permute-start.10) | collective-permute-done | bytes 524320 | tf_op jit(solution)/shard_map/ppermute | solution.py:351
  143.4 0.1 add_convert_fusion.1
  143.5 26.4 %all_to_all.15 = bf16[128,8,128]{2,1,0:T(8,128)(2,1)S(1)} all-to-all(bf16[128,8,128]{2,1,0:T(8,128)(2,1)S(1)} %bitcast.60), channel_id=1, replica_groups=mesh['zb'=2,'za'=2,'x'=4,'c'=2,'y'=4,'zh'=2] {'zb','za','x','y','zh'}, dimensions={0} | all-to-all | bytes 524288 | tf_op jit(solution)/shard_map/all_to_all | solution.py:352
  169.9 0.1 convert_reduce_fusion
  170.1 0.1 fusion.16
  170.1 0.6 pad_maximum_fusion.3
  (22 shorter events, 0.2 us)
Async XLA Ops:
  0.0 12.1 %copy-start = (s32[32,1]{0,1:T(1,128)S(1)}, s32[32,1]{0,1:T(1,128)}, u32[]{:S(2)}) copy-start(s32[32,1]{0,1:T(1,128)} %param.15) | copy-start | bytes 388
  3.3 9.5 %copy-start.1 = (bf16[8,128,256]{2,1,0:T(8,128)(2,1)S(1)}, bf16[8,128,256]{2,1,0:T(8,128)(2,1)}, u32[]{:S(2)}) copy-start(bf16[8,128,256]{2,1,0:T(8,128)(2,1)} %own.1) | copy-start | bytes 1572868
  3.3 70.3 %all-to-all-start = ((bf16[16,680,128]{2,1,0:T(8,128)(2,1)}), bf16[16,680,128]{2,1,0:T(8,128)(2,1)S(1)}, u32[]{:S(2)}, u32[]{:S(2)}) async-start(bf16[16,680,128]{2,1,0:T(8,128)(2,1)} %coef_payload.1), calls=%async_computation | async-start | bytes 5570560 | tf_op jit(solution)/shard_map/all_to_all | solution.py:288
  14.4 4.4 %collective-permute-start = (bf16[16,128,256]{2,1,0:T(8,128)(2,1)}, bf16[16,128,256]{2,1,0:T(8,128)(2,1)}, u32[]{:S(2)}, u32[]{:S(2)}) collective-permute-start(bf16[16,128,256]{2,1,0:T(8,128)(2,1)} %gather_fusion.3), channel_id=1, source_target_pairs={{0,8},{8,0},{1,9},{9,1},{2,10},{10,2},{3,11},{11,3},{4,12},{12,4},... | collective-permute-start | bytes 3145736 | tf_op jit(solution)/shard_map/ppermute | solution.py:295
  21.6 29.1 %collective-permute-start.1 = (bf16[2,4,128,256]{3,2,1,0:T(8,128)(2,1)}, bf16[2,4,128,256]{3,2,1,0:T(8,128)(2,1)}, u32[]{:S(2)}, u32[]{:S(2)}) collective-permute-start(bf16[2,4,128,256]{3,2,1,0:T(8,128)(2,1)} %pad_maximum_fusion), channel_id=1, source_target_pairs={{0,16},{16,32},{32,48},{48,0},{1,17},{17,33},{33,49},{49,1},{2,18}... | collective-permute-start | bytes 1572872 | tf_op jit(solution)/shard_map/ppermute | solution.py:267
  24.0 41.9 %collective-permute-start.2 = (bf16[2,4,128,256]{3,2,1,0:T(8,128)(2,1)}, bf16[2,4,128,256]{3,2,1,0:T(8,128)(2,1)}, u32[]{:S(2)}, u32[]{:S(2)}) collective-permute-start(bf16[2,4,128,256]{3,2,1,0:T(8,128)(2,1)} %pad_maximum_fusion.1), channel_id=1, source_target_pairs={{0,32},{16,48},{32,0},{48,16},{1,33},{17,49},{33,1},{49,17},{2,34}... | collective-permute-start | bytes 1572872 | tf_op jit(solution)/shard_map/ppermute | solution.py:267
  27.5 38.4 %collective-permute-start.3 = (bf16[2,4,128,256]{3,2,1,0:T(8,128)(2,1)}, bf16[2,4,128,256]{3,2,1,0:T(8,128)(2,1)}, u32[]{:S(2)}, u32[]{:S(2)}) collective-permute-start(bf16[2,4,128,256]{3,2,1,0:T(8,128)(2,1)} %pad_maximum_fusion.2), channel_id=1, source_target_pairs={{0,48},{16,0},{32,16},{48,32},{1,49},{17,1},{33,17},{49,33},{2,50}... | collective-permute-start | bytes 1572872 | tf_op jit(solution)/shard_map/ppermute | solution.py:267
  73.6 7.2 %collective-permute-start.4 = (bf16[16,680,128]{2,1,0:T(8,128)(2,1)S(1)}, bf16[16,680,128]{2,1,0:T(8,128)(2,1)}, u32[]{:S(2)}, u32[]{:S(2)}) collective-permute-start(bf16[16,680,128]{2,1,0:T(8,128)(2,1)S(1)} %all-to-all-done.mine), channel_id=1, source_target_pairs={{0,8},{8,0},{1,9},{9,1},{2,10},{10,2},{3,11},{11,3},{4,12},{12,4},... | collective-permute-start | bytes 8355848 | tf_op jit(solution)/shard_map/ppermute | solution.py:310
  73.6 59.7 %all-to-all-start.1 = ((bf16[32,128,256]{2,1,0:T(8,128)(2,1)}), bf16[32,128,256]{2,1,0:T(8,128)(2,1)}, u32[]{:S(2)}, u32[]{:S(2)}) async-start(bf16[32,128,256]{2,1,0:T(8,128)(2,1)} %bitcast.59), calls=%async_computation.1 | async-start | bytes 4194304 | tf_op jit(solution)/shard_map/all_to_all | solution.py:308
  85.6 14.9 %copy-start.3 = (s32[8,12]{1,0:T(8,128)S(1)}, s32[8,12]{1,0:T(8,128)}, u32[]{:S(2)}) copy-start(s32[8,12]{1,0:T(8,128)} %refs_1_.1) | copy-start | bytes 1156
  85.6 14.7 %collective-permute-start.5 = (bf16[4,384,128]{2,1,0:T(8,128)(2,1)S(1)}, bf16[4,384,128]{2,1,0:T(8,128)(2,1)S(1)}, u32[]{:S(2)}, u32[]{:S(2)}) collective-permute-start(bf16[4,384,128]{2,1,0:T(8,128)(2,1)S(1)} %density_partials.3), channel_id=1, source_target_pairs={{0,16},{16,32},{32,48},{48,0},{1,17},{17,33},{33,49},{49,1},{2,18}... | collective-permute-start | bytes 1179656 | tf_op jit(solution)/shard_map/ppermute | solution.py:267
  97.3 3.1 %copy-start.2 = (bf16[4,384,128]{2,1,0:T(8,128)(2,1)}, bf16[4,384,128]{2,1,0:T(8,128)(2,1)S(1)}, u32[]{:S(2)}) copy-start(bf16[4,384,128]{2,1,0:T(8,128)(2,1)S(1)} %get-tuple-element.17) | copy-start | bytes 1179652
  97.3 11.4 %collective-permute-start.7 = (bf16[4,384,128]{2,1,0:T(8,128)(2,1)}, bf16[4,384,128]{2,1,0:T(8,128)(2,1)S(1)}, u32[]{:S(2)}, u32[]{:S(2)}) collective-permute-start(bf16[4,384,128]{2,1,0:T(8,128)(2,1)} %get-tuple-element.19), channel_id=1, source_target_pairs={{0,48},{16,0},{32,16},{48,32},{1,49},{17,1},{33,17},{49,33},{2,50}... | collective-permute-start | bytes 1179656 | tf_op jit(solution)/shard_map/ppermute | solution.py:267
  100.4 11.7 %collective-permute-start.6 = (bf16[4,384,128]{2,1,0:T(8,128)(2,1)S(1)}, bf16[4,384,128]{2,1,0:T(8,128)(2,1)S(1)}, u32[]{:S(2)}, u32[]{:S(2)}) collective-permute-start(bf16[4,384,128]{2,1,0:T(8,128)(2,1)S(1)} %add_convert_fusion), channel_id=1, source_target_pairs={{0,16},{16,32},{32,48},{48,0},{1,17},{17,33},{33,49},{49,1},{2,18}... | collective-permute-start | bytes 1179656 | tf_op jit(solution)/shard_map/ppermute | solution.py:267
  113.2 6.8 %collective-permute-start.8 = (bf16[2,384,128]{2,1,0:T(8,128)(2,1)S(1)}, bf16[2,384,128]{2,1,0:T(8,128)(2,1)S(1)}, u32[]{:S(2)}, u32[]{:S(2)}) collective-permute-start(bf16[2,384,128]{2,1,0:T(8,128)(2,1)S(1)} %slice.149), channel_id=1, source_target_pairs={{0,64},{64,0},{1,65},{65,1},{2,66},{66,2},{3,67},{67,3},{4,68},{68... | collective-permute-start | bytes 589832 | tf_op jit(solution)/shard_map/ppermute | solution.py:318
  120.1 14.9 %collective-permute-start.9 = (bf16[384,128]{1,0:T(8,128)(2,1)S(1)}, bf16[384,128]{1,0:T(8,128)(2,1)S(1)}, u32[]{:S(2)}, u32[]{:S(2)}) collective-permute-start(bf16[384,128]{1,0:T(8,128)(2,1)S(1)} %get-tuple-element.23), channel_id=1, source_target_pairs={{0,128},{128,0},{1,129},{129,1},{2,130},{130,2},{3,131},{131,3},{4... | collective-permute-start | bytes 294920 | tf_op jit(solution)/shard_map/ppermute | solution.py:320
  141.4 2.0 %collective-permute-start.10 = (f32[16,8,8,128]{3,2,1,0:T(8,128)S(1)}, f32[16,8,8,128]{3,2,1,0:T(8,128)S(1)}, u32[]{:S(2)}, u32[]{:S(2)}) collective-permute-start(f32[16,8,8,128]{3,2,1,0:T(8,128)S(1)} %get-tuple-element.22), channel_id=1, source_target_pairs={{0,8},{8,0},{1,9},{9,1},{2,10},{10,2},{3,11},{11,3},{4,12},{12,4},... | collective-permute-start | bytes 1572872 | tf_op jit(solution)/shard_map/ppermute | solution.py:351

commit v5 on v4

--- a/solution.py
+++ b/solution.py
@@ -58,35 +58,40 @@
 
 
 def payload_kernel(occ, vir, *refs):
-    given, (out, occ_in, vir_in, packed, *small, sems_in, sems_out) = refs[:3], refs[3:]
-    copies = [pltpu.make_async_copy(given[n], small[n], sems_in.at[NS, n]) for n in range(3)]
+    given, (out, occ_in, vir_in, packed, table, *small, sems_in, sems_out) = refs[:3], refs[3:]
+    copies = [pltpu.make_async_copy(given[n], small[n], sems_in.at[LOCAL, n]) for n in range(3)]
     for copy in copies:
         copy.start()
     loads, stores = [], []
-    for s in range(NS):
+    for blk in range(LOCAL):
+        rows = pl.ds(blk * BB, BB)
         loads.append(
             (
-                pltpu.make_async_copy(occ.at[:, pl.ds(s * KO, KO)], occ_in.at[s], sems_in.at[s, 0]),
-                pltpu.make_async_copy(vir.at[:, pl.ds(s * KV, KV)], vir_in.at[s], sems_in.at[s, 1]),
+                pltpu.make_async_copy(occ.at[rows], occ_in.at[rows], sems_in.at[blk, 0]),
+                pltpu.make_async_copy(vir.at[rows], vir_in.at[rows], sems_in.at[blk, 1]),
             )
         )
         for load in loads[-1]:
             load.start()
-    for copy in copies:
-        copy.wait()
-    table = table_of(*small)
-    for s in range(NS):
-        for load in loads[s]:
+    for blk in range(LOCAL):
+        for load in loads[blk]:
             load.wait()
-        for blk in range(LOCAL):
-            rows = slice(blk * BB, (blk + 1) * BB)
+        rows = slice(blk * BB, (blk + 1) * BB)
+        for s in range(NS):
             for kt in range(KT):
-                at = blk * BLK + kt * BB
-                stage, first = (occ_in, kt) if kt < TO else (vir_in, kt - TO)
-                packed[s, at : at + BB, :] = stage[s, rows, first * LANES : (first + 1) * LANES]
-        packed[s, LOCAL * BLK : PAY, :] = table
-        stores.append(pltpu.make_async_copy(packed.at[s], out.at[s], sems_out.at[s]))
+                stage, first = (occ_in, s * TO + kt) if kt < TO else (vir_in, s * TV + kt - TO)
+                tile = stage[rows, first * LANES : (first + 1) * LANES]
+                packed[blk, s, kt * BB : (kt + 1) * BB, :] = tile
+        place = out.at[:, pl.ds(blk * BLK, BLK)]
+        stores.append(pltpu.make_async_copy(packed.at[blk], place, sems_out.at[blk]))
         stores[-1].start()
+        if blk == 2:
+            for copy in copies:
+                copy.wait()
+            table[...] = jnp.broadcast_to(table_of(*small)[None], (NS, 8, LANES))
+            rest = out.at[:, pl.ds(LOCAL * BLK, 8)]
+            stores.append(pltpu.make_async_copy(table, rest, sems_out.at[LOCAL]))
+            stores[-1].start()
     for store in stores:
         store.wait()
 
@@ -99,12 +104,13 @@
         in_specs=[hbm] * 5,
         out_specs=hbm,
         scratch_shapes=[
-            pltpu.VMEM((NS, ROWS, KO), bf16),
-            pltpu.VMEM((NS, ROWS, KV), bf16),
-            pltpu.VMEM((NS, PAY, LANES), bf16),
+            pltpu.VMEM((ROWS, NS * KO), bf16),
+            pltpu.VMEM((ROWS, NS * KV), bf16),
+            pltpu.VMEM((LOCAL, NS, BLK, LANES), bf16),
+            pltpu.VMEM((NS, 8, LANES), bf16),
         ]
         + [pltpu.VMEM(part.shape, part.dtype) for part in extra]
-        + [pltpu.SemaphoreType.DMA((NS + 1, 3)), pltpu.SemaphoreType.DMA((NS,))],
+        + [pltpu.SemaphoreType.DMA((LOCAL + 1, 3)), pltpu.SemaphoreType.DMA((LOCAL + 1,))],
         compiler_params=pltpu.CompilerParams(vmem_limit_bytes=60 << 20),
         cost_estimate=pl.CostEstimate(flops=0, bytes_accessed=6 << 20, transcendentals=0),
         name="coef_payload",
@@ -200,17 +206,13 @@
 
 
 def tile_kernel(
-    meta, kept, moved, blocks, own, keep, give, recv, dens, *refs
+    meta, kept, moved, recv, own, keep, give, dens, *refs
 ):
-    occs, virs, krons, accs, (chi, sem) = refs[0:4], refs[4:8], refs[8:12], refs[12:16], refs[16:]
-    load = pltpu.make_async_copy(blocks, recv, sem)
-    load.start()
+    occs, virs, krons, accs, (chi,) = refs[0:8], refs[8:16], refs[16:24], refs[24:32], refs[32:]
     dens[...] = (kept[...] + moved[...].astype(f32)).astype(bf16)
     chi[...] = jnp.zeros_like(chi)
     row = lax.broadcasted_iota(jnp.int32, (NJ * BB, BB * BB), 0)
     col = lax.broadcasted_iota(jnp.int32, (NJ * BB, BB * BB), 1)
-
-    load.wait()
 
     def expand(j, occ_exp, vir_exp, acc):
         hot_occ = (row == j * BB + col // BB).astype(f32).astype(bf16)
@@ -236,17 +238,17 @@
             own[j], rows, (((1,), (1,)), ((), ())), preferred_element_type=f32
         )
 
-    def per_four(i, carry):
-        for n in range(4):
-            expand(4 * i + n, occs[n], virs[n], accs[n])
+    def per_all(i, carry):
+        for n in range(8):
+            expand(8 * i + n, occs[n], virs[n], accs[n])
         for t in range(NNB):
-            for n in range(4):
-                add_partner(4 * i + n, t, occs[n], virs[n], krons[n], accs[n])
-        for n in range(4):
-            finish(4 * i + n, accs[n])
+            for n in range(8):
+                add_partner(8 * i + n, t, occs[n], virs[n], krons[n], accs[n])
+        for n in range(8):
+            finish(8 * i + n, accs[n])
         return carry
 
-    lax.fori_loop(0, NJ // 4, per_four, 0)
+    lax.fori_loop(0, NJ // 8, per_all, 0)
     low = lax.broadcasted_iota(jnp.int32, (1, 8, 128), 2) < 64
     first = jnp.full((1, 8, 128), meta[248], jnp.int32) == 0
     for tile in range(4):
@@ -282,7 +284,6 @@
     share = zl * NX + x
     vmem = pl.BlockSpec(memory_space=pltpu.VMEM)
     smem = pl.BlockSpec(memory_space=pltpu.SMEM)
-    whole = pl.BlockSpec(memory_space=pl.ANY)
     spread_out = functools.partial(lax.all_to_all, split_axis=0, concat_axis=0, tiled=True)
     extra = (pair_blocks.T, partners, partner_blocks.transpose(2, 0, 1))
     mine = spread_out(payload_call(occ_coef, vir_coef, extra), ZX)
@@ -331,16 +332,15 @@
     keep, give = pl.pallas_call(
         tile_kernel,
         out_shape=(out_half, out_half),
-        in_specs=[smem, vmem, vmem, whole, vmem],
+        in_specs=[smem, vmem, vmem, vmem, vmem],
         out_specs=(vmem, vmem),
         scratch_shapes=[
-            pltpu.VMEM((32, AB, BB * BB), bf16),
             pltpu.VMEM((2 * TR, NJ * BB), bf16),
         ]
-        + [pltpu.VMEM((TR, BB * BB), f32)] * 8
-        + [pltpu.VMEM((2, BB * BB, BB * BB), bf16)] * 4
-        + [pltpu.VMEM((NAB, AB, BB * BB), f32)] * 4
-        + [pltpu.VMEM((NAB, AB, NAB * AB), f32), pltpu.SemaphoreType.DMA],
+        + [pltpu.VMEM((TR, BB * BB), f32)] * 16
+        + [pltpu.VMEM((2, BB * BB, BB * BB), bf16)] * 8
+        + [pltpu.VMEM((NAB, AB, BB * BB), f32)] * 8
+        + [pltpu.VMEM((NAB, AB, NAB * AB), f32)],
         compiler_params=pltpu.CompilerParams(vmem_limit_bytes=32 << 20),
         cost_estimate=pl.CostEstimate(
             flops=2 * 96 * 128 * 256 * 256, bytes_accessed=4 << 20, transcendentals=0

time: 171 us -> 171 us (level)
  no operation moved by 1% of the time
where the time goes in v5:
time: 171 us; the launch traced here: 170 us
  waiting for transfers between devices  59.7 us (35%)
  starting transfers between devices  37.7 us (22%)
  blocking collectives  26.4 us (15%)
  Pallas kernels  24.8 us (15%)
  local copies, waits for them, and re-layouts  13.4 us (8%)
  other arithmetic  7.69 us (4%)
    ppermute x6, waiting for transfers between devices, shift(): lax.ppermute(rows, axis, [(i, (i + k) % size) for i in range(size)])  45.7 us
    all_to_all x1, blocking collectives, body(): lax.all_to_all(pair_sum.astype(bf16).reshape(128, 8, 128), ZX + ('y', 'zh...  26.4 us
    pallas_call x2, Pallas kernels, dens_call(): pl.pallas_call(functools.partial(dens_kernel, jobs), out_shape=(part,) *...  15.9 us
    ppermute x1, starting transfers between devices, body(): lax.ppermute((summed[1] + crossed[1]).astype(bf16), 'zb', flip)  12.3 us
    ppermute x6, starting transfers between devices, shift(): lax.ppermute(rows, axis, [(i, (i + k) % size) for i in range(size)])  9.19 us
    all_to_all x1, starting transfers between devices, body(): mine = spread_out(payload_call(occ_coef, vir_coef, extra), ZX)  8.63 us
    all_to_all x1, starting transfers between devices, body(): received = spread_out(by_z, ZL)  7.17 us
    pallas_call x1, Pallas kernels, body(): pl.pallas_call(tile_kernel, out_shape=(out_half, out_half), in_specs=[sme...  5.74 us
  transfers between devices with their start and end apart: 13, of which 8 were waited for; matrix products, arithmetic and copies ran while one was open for 12% of the time, Pallas kernels for 9%

profile of v5, /device:TPU:32, one launch (start us, length us, event | category | flops | bytes accessed | tf_op | source)
XLA Modules:
  0.0 169.9 jit_solution(1212050809106301962)
XLA Ops:
  0.0 0.0 copy-start
  0.0 3.1 %coef_payload.1 = bf16[16,680,128]{2,1,0:T(8,128)(2,1)} custom-call(bf16[96,4096]{1,0:T(8,128)(2,1)} %occ.1, bf16[96,10240]{1,0:T(8,128)(2,1)} %vir.1, s32[3,8]{1,0:T(4,128)} %bitcast.62, s32[8,12]{1,0:T(8,128)} %refs_1_.1, s32[3,8,12]{2,1,0:T(8,128)} %bitcast.61), custom_call_target="tpu_custom_call" | custom-call | bytes 6291456 | tf_op jit(solution)/shard_map/coef_payload/pallas_call | solution.py:101
  3.1 0.0 copy-start.1
  3.2 8.6 %all-to-all-start = ((bf16[16,680,128]{2,1,0:T(8,128)(2,1)}), bf16[16,680,128]{2,1,0:T(8,128)(2,1)S(1)}, u32[]{:S(2)}, u32[]{:S(2)}) async-start(bf16[16,680,128]{2,1,0:T(8,128)(2,1)} %coef_payload.1), calls=%async_computation | async-start | bytes 5570560 | tf_op jit(solution)/shard_map/all_to_all | solution.py:289
  11.8 0.1 add_add_fusion.1
  11.9 0.1 sub.36
  12.0 0.7 gather_fusion.2
  12.7 0.0 copy-done.1
  12.7 1.6 gather_fusion.3
  14.3 0.0 collective-permute-start
  14.3 0.1 add.185
  14.4 0.7 gather_fusion
  15.0 1.6 gather_fusion.1
  16.7 2.0 %slice_bitcast_fusion.7 = (bf16[1,4,128,256]{3,2,1,0:T(8,128)(2,1)}, bf16[1,4,128,256]{3,2,1,0:T(8,128)(2,1)S(1)}, bf16[1,4,128,256]{3,2,1,0:T(8,128)(2,1)S(1)}, bf16[1,4,128,256]{3,2,1,0:T(8,128)(2,1)S(1)}) fusion(bf16[16,128,256]{2,1,0:T(8,128)(2,1)} %gather_fusion.1), kind=kLoop, calls=%fused_computation.21 | loop fusion | bytes 2097152 | tf_op jit(solution)/shard_map/slice | solution.py:299
  18.6 0.0 collective-permute-done
  18.7 2.0 %slice_bitcast_fusion.6 = (bf16[1,4,128,256]{3,2,1,0:T(8,128)(2,1)}, bf16[1,4,128,256]{3,2,1,0:T(8,128)(2,1)S(1)}, bf16[1,4,128,256]{3,2,1,0:T(8,128)(2,1)S(1)}, bf16[1,4,128,256]{3,2,1,0:T(8,128)(2,1)S(1)}) fusion(bf16[16,128,256]{2,1,0:T(8,128)(2,1)} %collective-permute-done), kind=kLoop, calls=%fused_computation.20 | loop fusion | bytes 2097152 | tf_op jit(solution)/shard_map/slice | solution.py:299
  20.6 0.9 pad_maximum_fusion
  21.5 1.5 collective-permute-start.1
  23.0 0.9 pad_maximum_fusion.1
  23.8 2.7 %collective-permute-start.2 = (bf16[2,4,128,256]{3,2,1,0:T(8,128)(2,1)}, bf16[2,4,128,256]{3,2,1,0:T(8,128)(2,1)}, u32[]{:S(2)}, u32[]{:S(2)}) collective-permute-start(bf16[2,4,128,256]{3,2,1,0:T(8,128)(2,1)} %pad_maximum_fusion.1), channel_id=1, source_target_pairs={{0,32},{16,48},{32,0},{48,16},{1,33},{17,49},{33,1},{49,17},{2,34}... | collective-permute-start | bytes 1572872 | tf_op jit(solution)/shard_map/ppermute | solution.py:269
  26.5 0.8 pad_maximum_fusion.2
  27.4 1.5 collective-permute-start.3
  28.8 0.8 dynamic_slice.6
  29.6 0.8 dynamic_slice.7
  30.4 0.1 pad_add_fusion.pos
  30.4 1.1 maximum_bitcast_fusion.1
  31.5 19.1 %collective-permute-done.1 = bf16[2,4,128,256]{3,2,1,0:T(8,128)(2,1)} collective-permute-done((bf16[2,4,128,256]{3,2,1,0:T(8,128)(2,1)}, bf16[2,4,128,256]{3,2,1,0:T(8,128)(2,1)}, u32[]{:S(2)}, u32[]{:S(2)}) %collective-permute-start.1) | collective-permute-done | bytes 524320 | tf_op jit(solution)/shard_map/ppermute | solution.py:269
  50.6 15.1 %collective-permute-done.2 = bf16[2,4,128,256]{3,2,1,0:T(8,128)(2,1)} collective-permute-done((bf16[2,4,128,256]{3,2,1,0:T(8,128)(2,1)}, bf16[2,4,128,256]{3,2,1,0:T(8,128)(2,1)}, u32[]{:S(2)}, u32[]{:S(2)}) %collective-permute-start.2) | collective-permute-done | bytes 524320 | tf_op jit(solution)/shard_map/ppermute | solution.py:269
  65.7 0.0 collective-permute-done.3
  65.7 1.6 maximum_bitcast_fusion
  67.3 1.5 copy.11
  68.8 4.6 %all-to-all-done.mine = bf16[16,680,128]{2,1,0:T(8,128)(2,1)S(1)} async-done(((bf16[16,680,128]{2,1,0:T(8,128)(2,1)}), bf16[16,680,128]{2,1,0:T(8,128)(2,1)S(1)}, u32[]{:S(2)}, u32[]{:S(2)}) %all-to-all-start) | async-done | bytes 2785312 | tf_op jit(solution)/shard_map/all_to_all | solution.py:289
  73.5 0.0 collective-permute-start.4
  73.5 7.2 %all-to-all-start.1 = ((bf16[32,128,256]{2,1,0:T(8,128)(2,1)}), bf16[32,128,256]{2,1,0:T(8,128)(2,1)}, u32[]{:S(2)}, u32[]{:S(2)}) async-start(bf16[32,128,256]{2,1,0:T(8,128)(2,1)} %bitcast.59), calls=%async_computation.1 | async-start | bytes 4194304 | tf_op jit(solution)/shard_map/all_to_all | solution.py:309
  80.7 0.0 collective-permute-done.4.other
  80.7 4.8 %density_partials.3 = bf16[4,384,128]{2,1,0:T(8,128)(2,1)S(1)} custom-call(s32[128,128]{1,0:T(8,128)S(1)} %bitcast_convert_fusion.tab, s32[4]{0:T(128)S(1)} %pad_add_fusion.pos, bf16[16,680,128]{2,1,0:T(8,128)(2,1)S(1)} %all-to-all-done.mine, bf16[16,680,128]{2,1,0:T(8,128)(2,1)} %collective-permute-done.4.other, f32[7,128]{1,0:T(8,128)S(1)} %maximum_bitcast_fusion.2.wts), custom_call_target="tpu_custom_call" | custom-call | flops 469762048 | bytes 6291456 | tf_op jit(solution)/shard_map/density_partials/pallas_call | solution.py:187
  85.5 0.0 copy-start.3
  85.5 0.6 collective-permute-start.5
  86.0 11.1 %density_partials.2 = (bf16[4,384,128]{2,1,0:T(8,128)(2,1)S(1)}, bf16[4,384,128]{2,1,0:T(8,128)(2,1)}, bf16[4,384,128]{2,1,0:T(8,128)(2,1)S(1)}) custom-call(s32[128,128]{1,0:T(8,128)S(1)} %bitcast_convert_fusion.tab, s32[4]{0:T(128)S(1)} %pad_add_fusion.pos, bf16[16,680,128]{2,1,0:T(8,128)(2,1)S(1)} %all-to-all-done.mine, ...), custom_call_target="tpu_custom_call" | custom-call | flops 1409286144 | bytes 6291456 | tf_op jit(solution)/shard_map/density_partials/pallas_call | solution.py:187
  97.1 3.0 %collective-permute-start.7 = (bf16[4,384,128]{2,1,0:T(8,128)(2,1)}, bf16[4,384,128]{2,1,0:T(8,128)(2,1)S(1)}, u32[]{:S(2)}, u32[]{:S(2)}) collective-permute-start(bf16[4,384,128]{2,1,0:T(8,128)(2,1)} %get-tuple-element.19), channel_id=1, source_target_pairs={{0,48},{16,0},{32,16},{48,32},{1,49},{17,1},{33,17},{49,33},{2,50}... | collective-permute-start | bytes 1179656 | tf_op jit(solution)/shard_map/ppermute | solution.py:269
  100.1 0.0 collective-permute-done.5
  100.1 0.1 add_convert_fusion
  100.2 0.1 collective-permute-start.6
  100.3 0.1 reshape.152
  100.4 8.2 %collective-permute-done.7 = bf16[4,384,128]{2,1,0:T(8,128)(2,1)S(1)} collective-permute-done((bf16[4,384,128]{2,1,0:T(8,128)(2,1)}, bf16[4,384,128]{2,1,0:T(8,128)(2,1)S(1)}, u32[]{:S(2)}, u32[]{:S(2)}) %collective-permute-start.7) | collective-permute-done | bytes 393248 | tf_op jit(solution)/shard_map/ppermute | solution.py:269
  108.6 3.3 %collective-permute-done.6 = bf16[4,384,128]{2,1,0:T(8,128)(2,1)S(1)} collective-permute-done((bf16[4,384,128]{2,1,0:T(8,128)(2,1)S(1)}, bf16[4,384,128]{2,1,0:T(8,128)(2,1)S(1)}, u32[]{:S(2)}, u32[]{:S(2)}) %collective-permute-start.6) | collective-permute-done | bytes 393248 | tf_op jit(solution)/shard_map/ppermute | solution.py:269
  111.9 1.2 convert_add_fusion
  113.1 0.4 collective-permute-start.8
  113.5 0.7 slice_bitcast_fusion.8
  114.2 5.7 %collective-permute-done.8 = bf16[2,384,128]{2,1,0:T(8,128)(2,1)S(1)} collective-permute-done((bf16[2,384,128]{2,1,0:T(8,128)(2,1)S(1)}, bf16[2,384,128]{2,1,0:T(8,128)(2,1)S(1)}, u32[]{:S(2)}, u32[]{:S(2)}) %collective-permute-start.8) | collective-permute-done | bytes 196640 | tf_op jit(solution)/shard_map/ppermute | solution.py:319
  120.0 12.3 %collective-permute-start.9 = (bf16[384,128]{1,0:T(8,128)(2,1)S(1)}, bf16[384,128]{1,0:T(8,128)(2,1)S(1)}, u32[]{:S(2)}, u32[]{:S(2)}) collective-permute-start(bf16[384,128]{1,0:T(8,128)(2,1)S(1)} %get-tuple-element.23), channel_id=1, source_target_pairs={{0,128},{128,0},{1,129},{129,1},{2,130},{130,2},{3,131},{131,3},{4... | collective-permute-start | bytes 294920 | tf_op jit(solution)/shard_map/ppermute | solution.py:321
  132.3 0.7 slice.79
  133.0 0.1 reshape_squeeze.3
  133.1 0.1 concatenate.9.meta
  133.2 0.0 all-to-all-done.1.recv
  133.2 1.7 collective-permute-done.9.moved
  134.9 5.7 %chi_tiles.1 = (f32[16,8,8,128]{3,2,1,0:T(8,128)S(1)}, f32[16,8,8,128]{3,2,1,0:T(8,128)S(1)}) custom-call(s32[256]{0:T(256)S(1)} %concatenate.9.meta, f32[384,128]{1,0:T(8,128)S(1)} %get-tuple-element.24.kept, bf16[384,128]{1,0:T(8,128)(2,1)S(1)} %collective-permute-done.9.moved, bf16[32,128,256]{2,1,0:T(8,128)(2,1)} %all-to-all-done.1.recv, ...), custom_call_target="tpu_custom_call" | custom-call | flops 1610612736 | bytes 4194304 | tf_op jit(solution)/shard_map/chi_tiles/pallas_call | solution.py:332
  140.6 0.1 collective-permute-start.10
  140.7 1.9 %collective-permute-done.10 = f32[16,8,8,128]{3,2,1,0:T(8,128)S(1)} collective-permute-done((f32[16,8,8,128]{3,2,1,0:T(8,128)S(1)}, f32[16,8,8,128]{3,2,1,0:T(8,128)S(1)}, u32[]{:S(2)}, u32[]{:S(2)}) %collective-permute-start.10) | collective-permute-done | bytes 524320 | tf_op jit(solution)/shard_map/ppermute | solution.py:351
  142.6 0.1 add_convert_fusion.1
  142.7 26.4 %all_to_all.15 = bf16[128,8,128]{2,1,0:T(8,128)(2,1)S(1)} all-to-all(bf16[128,8,128]{2,1,0:T(8,128)(2,1)S(1)} %bitcast.60), channel_id=1, replica_groups=mesh['zb'=2,'za'=2,'x'=4,'c'=2,'y'=4,'zh'=2] {'zb','za','x','y','zh'}, dimensions={0} | all-to-all | bytes 524288 | tf_op jit(solution)/shard_map/all_to_all | solution.py:352
  169.1 0.1 convert_reduce_fusion
  169.2 0.1 fusion.16
  169.3 0.6 pad_maximum_fusion.3
  (22 shorter events, 0.2 us)
Async XLA Ops:
  0.0 12.0 %copy-start = (s32[32,1]{0,1:T(1,128)S(1)}, s32[32,1]{0,1:T(1,128)}, u32[]{:S(2)}) copy-start(s32[32,1]{0,1:T(1,128)} %param.15) | copy-start | bytes 388
  3.1 9.5 %copy-start.1 = (bf16[8,128,256]{2,1,0:T(8,128)(2,1)S(1)}, bf16[8,128,256]{2,1,0:T(8,128)(2,1)}, u32[]{:S(2)}) copy-start(bf16[8,128,256]{2,1,0:T(8,128)(2,1)} %own.1) | copy-start | bytes 1572868
  3.2 70.3 %all-to-all-start = ((bf16[16,680,128]{2,1,0:T(8,128)(2,1)}), bf16[16,680,128]{2,1,0:T(8,128)(2,1)S(1)}, u32[]{:S(2)}, u32[]{:S(2)}) async-start(bf16[16,680,128]{2,1,0:T(8,128)(2,1)} %coef_payload.1), calls=%async_computation | async-start | bytes 5570560 | tf_op jit(solution)/shard_map/all_to_all | solution.py:289
  14.3 4.4 %collective-permute-start = (bf16[16,128,256]{2,1,0:T(8,128)(2,1)}, bf16[16,128,256]{2,1,0:T(8,128)(2,1)}, u32[]{:S(2)}, u32[]{:S(2)}) collective-permute-start(bf16[16,128,256]{2,1,0:T(8,128)(2,1)} %gather_fusion.3), channel_id=1, source_target_pairs={{0,8},{8,0},{1,9},{9,1},{2,10},{10,2},{3,11},{11,3},{4,12},{12,4},... | collective-permute-start | bytes 3145736 | tf_op jit(solution)/shard_map/ppermute | solution.py:296
  21.5 29.1 %collective-permute-start.1 = (bf16[2,4,128,256]{3,2,1,0:T(8,128)(2,1)}, bf16[2,4,128,256]{3,2,1,0:T(8,128)(2,1)}, u32[]{:S(2)}, u32[]{:S(2)}) collective-permute-start(bf16[2,4,128,256]{3,2,1,0:T(8,128)(2,1)} %pad_maximum_fusion), channel_id=1, source_target_pairs={{0,16},{16,32},{32,48},{48,0},{1,17},{17,33},{33,49},{49,1},{2,18}... | collective-permute-start | bytes 1572872 | tf_op jit(solution)/shard_map/ppermute | solution.py:269
  23.8 41.9 %collective-permute-start.2 = (bf16[2,4,128,256]{3,2,1,0:T(8,128)(2,1)}, bf16[2,4,128,256]{3,2,1,0:T(8,128)(2,1)}, u32[]{:S(2)}, u32[]{:S(2)}) collective-permute-start(bf16[2,4,128,256]{3,2,1,0:T(8,128)(2,1)} %pad_maximum_fusion.1), channel_id=1, source_target_pairs={{0,32},{16,48},{32,0},{48,16},{1,33},{17,49},{33,1},{49,17},{2,34}... | collective-permute-start | bytes 1572872 | tf_op jit(solution)/shard_map/ppermute | solution.py:269
  27.4 38.4 %collective-permute-start.3 = (bf16[2,4,128,256]{3,2,1,0:T(8,128)(2,1)}, bf16[2,4,128,256]{3,2,1,0:T(8,128)(2,1)}, u32[]{:S(2)}, u32[]{:S(2)}) collective-permute-start(bf16[2,4,128,256]{3,2,1,0:T(8,128)(2,1)} %pad_maximum_fusion.2), channel_id=1, source_target_pairs={{0,48},{16,0},{32,16},{48,32},{1,49},{17,1},{33,17},{49,33},{2,50}... | collective-permute-start | bytes 1572872 | tf_op jit(solution)/shard_map/ppermute | solution.py:269
  73.5 7.2 %collective-permute-start.4 = (bf16[16,680,128]{2,1,0:T(8,128)(2,1)S(1)}, bf16[16,680,128]{2,1,0:T(8,128)(2,1)}, u32[]{:S(2)}, u32[]{:S(2)}) collective-permute-start(bf16[16,680,128]{2,1,0:T(8,128)(2,1)S(1)} %all-to-all-done.mine), channel_id=1, source_target_pairs={{0,8},{8,0},{1,9},{9,1},{2,10},{10,2},{3,11},{11,3},{4,12},{12,4},... | collective-permute-start | bytes 8355848 | tf_op jit(solution)/shard_map/ppermute | solution.py:311
  73.5 59.7 %all-to-all-start.1 = ((bf16[32,128,256]{2,1,0:T(8,128)(2,1)}), bf16[32,128,256]{2,1,0:T(8,128)(2,1)}, u32[]{:S(2)}, u32[]{:S(2)}) async-start(bf16[32,128,256]{2,1,0:T(8,128)(2,1)} %bitcast.59), calls=%async_computation.1 | async-start | bytes 4194304 | tf_op jit(solution)/shard_map/all_to_all | solution.py:309
  85.5 14.9 %copy-start.3 = (s32[8,12]{1,0:T(8,128)S(1)}, s32[8,12]{1,0:T(8,128)}, u32[]{:S(2)}) copy-start(s32[8,12]{1,0:T(8,128)} %refs_1_.1) | copy-start | bytes 1156
  85.5 14.6 %collective-permute-start.5 = (bf16[4,384,128]{2,1,0:T(8,128)(2,1)S(1)}, bf16[4,384,128]{2,1,0:T(8,128)(2,1)S(1)}, u32[]{:S(2)}, u32[]{:S(2)}) collective-permute-start(bf16[4,384,128]{2,1,0:T(8,128)(2,1)S(1)} %density_partials.3), channel_id=1, source_target_pairs={{0,16},{16,32},{32,48},{48,0},{1,17},{17,33},{33,49},{49,1},{2,18}... | collective-permute-start | bytes 1179656 | tf_op jit(solution)/shard_map/ppermute | solution.py:269
  97.1 3.1 %copy-start.2 = (bf16[4,384,128]{2,1,0:T(8,128)(2,1)}, bf16[4,384,128]{2,1,0:T(8,128)(2,1)S(1)}, u32[]{:S(2)}) copy-start(bf16[4,384,128]{2,1,0:T(8,128)(2,1)S(1)} %get-tuple-element.17) | copy-start | bytes 1179652
  97.1 11.5 %collective-permute-start.7 = (bf16[4,384,128]{2,1,0:T(8,128)(2,1)}, bf16[4,384,128]{2,1,0:T(8,128)(2,1)S(1)}, u32[]{:S(2)}, u32[]{:S(2)}) collective-permute-start(bf16[4,384,128]{2,1,0:T(8,128)(2,1)} %get-tuple-element.19), channel_id=1, source_target_pairs={{0,48},{16,0},{32,16},{48,32},{1,49},{17,1},{33,17},{49,33},{2,50}... | collective-permute-start | bytes 1179656 | tf_op jit(solution)/shard_map/ppermute | solution.py:269
  100.2 11.7 %collective-permute-start.6 = (bf16[4,384,128]{2,1,0:T(8,128)(2,1)S(1)}, bf16[4,384,128]{2,1,0:T(8,128)(2,1)S(1)}, u32[]{:S(2)}, u32[]{:S(2)}) collective-permute-start(bf16[4,384,128]{2,1,0:T(8,128)(2,1)S(1)} %add_convert_fusion), channel_id=1, source_target_pairs={{0,16},{16,32},{32,48},{48,0},{1,17},{17,33},{33,49},{49,1},{2,18}... | collective-permute-start | bytes 1179656 | tf_op jit(solution)/shard_map/ppermute | solution.py:269
  113.1 6.8 %collective-permute-start.8 = (bf16[2,384,128]{2,1,0:T(8,128)(2,1)S(1)}, bf16[2,384,128]{2,1,0:T(8,128)(2,1)S(1)}, u32[]{:S(2)}, u32[]{:S(2)}) collective-permute-start(bf16[2,384,128]{2,1,0:T(8,128)(2,1)S(1)} %slice.149), channel_id=1, source_target_pairs={{0,64},{64,0},{1,65},{65,1},{2,66},{66,2},{3,67},{67,3},{4,68},{68... | collective-permute-start | bytes 589832 | tf_op jit(solution)/shard_map/ppermute | solution.py:319
  120.0 14.9 %collective-permute-start.9 = (bf16[384,128]{1,0:T(8,128)(2,1)S(1)}, bf16[384,128]{1,0:T(8,128)(2,1)S(1)}, u32[]{:S(2)}, u32[]{:S(2)}) collective-permute-start(bf16[384,128]{1,0:T(8,128)(2,1)S(1)} %get-tuple-element.23), channel_id=1, source_target_pairs={{0,128},{128,0},{1,129},{129,1},{2,130},{130,2},{3,131},{131,3},{4... | collective-permute-start | bytes 294920 | tf_op jit(solution)/shard_map/ppermute | solution.py:321
  140.6 2.0 %collective-permute-start.10 = (f32[16,8,8,128]{3,2,1,0:T(8,128)S(1)}, f32[16,8,8,128]{3,2,1,0:T(8,128)S(1)}, u32[]{:S(2)}, u32[]{:S(2)}) collective-permute-start(f32[16,8,8,128]{3,2,1,0:T(8,128)S(1)} %get-tuple-element.22), channel_id=1, source_target_pairs={{0,8},{8,0},{1,9},{9,1},{2,10},{10,2},{3,11},{11,3},{4,12},{12,4},... | collective-permute-start | bytes 1572872 | tf_op jit(solution)/shard_map/ppermute | solution.py:351
